TPU v7x, 32 devices: a whole 2x2x4 slice. The times are simulated.
32 devices in a mesh: parts: 2 (over x), expert: 16 (over z, y, core).
Axes of the slice: x: 2, y: 2, z: 4, core: 2. Of those that a mesh axis runs over, the one named last changes fastest.
Arguments:
- tokens: bfloat16 [2, 128, 7168], P(None, ('parts', 'expert')), parts along dimension 1, may hold values from -6 to 6
- live_rows: int32 [2, 32], P(None, ('parts', 'expert')), parts along dimension 1, may hold values from 3 to 4
- expert_ids: int32 [1, 2, 128, 8], P(None, None, ('parts', 'expert')), parts along dimension 2, may hold values from 0 to 15, all different within a row; in each aligned block of 4 rows (0 to 3, 4 to 7, ..., all dimensions but the last counted through in order) at most 2 rows name the same one
- gate_weights: float32 [1, 2, 128, 8], P(None, None, ('parts', 'expert')), parts along dimension 2, may hold values from 0.25 to 2.5
- norm_gain: float32 [1, 7168], replicated, may hold values from 0.1 to 1.9
- expert_gate_up: bfloat16 [1, 16, 7168, 2048], P(None, 'expert'), may hold values from -0.0625 to 0.0625
- expert_down: bfloat16 [1, 16, 1024, 7168], P(None, 'expert'), may hold values from -0.1875 to 0.1875
- shared_gate_up: bfloat16 [1, 7168, 2048], P(None, 'expert'), may hold values from -0.0625 to 0.0625
- shared_down: bfloat16 [1, 1024, 7168], P(None, None, 'expert'), may hold values from -0.1875 to 0.1875
Outputs:
- hidden_out: bfloat16 [2, 128, 7168], P(None, ('parts', 'expert')), parts along dimension 1
There are 2 independent parts, one for each index of `parts`. A program takes and returns all parts, laid end to end along the dimension named above; an argument that names none is the same for every part. Nothing has to cross between parts.
Inputs may be any that keep to these rules, and one draw needn't show every extreme that they name: `expert_ids`: the 8 ids of a row differ; within the rows of one device for one layer and step, no expert is named by more than 2 rows, a bound that some block reaches.
All inputs are finite; a program needn't handle non-finite values.
Results may differ from a plain program's by a relative error of at most 0.0068.
Values may be sent and summed in bfloat16 or wider, within the bound.
No kernel may reach another device: no remote copies, remote signals or barrier semaphores. Data moves between devices by JAX's collectives and lax.ppermute only.
A program may use at most 128 MiB of HBM per device.

v0:
```python
import functools
import math

import jax
import jax.numpy as jnp
from jax import lax
from jax.experimental import pallas as pl
from jax.experimental.pallas import tpu as pltpu
from jax.sharding import PartitionSpec as P


EXPERTS = 16
EPSILON = 1e-06
LANES = 128
SMALL_GRANT = 8 << 20
FIRST_EIGHTHS = 5
ROUTED_GRANT = 40 << 20
UP_STEP, UP_SLOTS = 512, 6
DOWN_STEP, DOWN_SLOTS = 896, 8


F32 = jnp.float32
BF16 = jnp.bfloat16


def vmem_spec():
    return pl.BlockSpec(memory_space=pltpu.VMEM)


def any_spec():
    return pl.BlockSpec(memory_space=pl.ANY)


def hbm_spec():
    return pl.BlockSpec(memory_space=pltpu.HBM)


def in_hbm(value):
    return pltpu.with_memory_space_constraint(value, pltpu.HBM)


def small_grant():
    return pltpu.CompilerParams(vmem_limit_bytes=SMALL_GRANT)


def largest_step(total, unit, limit):
    best = None
    for step in range(unit, limit + 1, unit):
        if total % step == 0:
            best = step
    return best if best is not None else total


def payload_kernel(expert_count, *refs):
    inputs, rest = refs[:5], refs[5:]
    out_ref, near, sems = rest[0], rest[1:6], rest[6]
    copies = [pltpu.make_async_copy(inputs[at], near[at], sems.at[at]) for at in range(5)]
    for copy in copies:
        copy.start()
    for copy in copies:
        copy.wait()
    live_ref, tokens_ref, ids_ref, gates_ref, gain_ref = near
    step_count, row_count, width = tokens_ref.shape
    top_count = ids_ref.shape[3]
    lane = lax.broadcasted_iota(jnp.int32, (row_count, LANES), 1)
    position = lax.broadcasted_iota(jnp.int32, (row_count, LANES), 0)
    third = jnp.where(lane >= 2 * expert_count, 2, jnp.where(lane >= expert_count, 1, 0))
    named = lane - third * expert_count
    for step_at in range(step_count):
        rows = pl.ds(step_at * row_count, row_count)
        widened = tokens_ref[step_at].astype(F32)
        scaling = lax.rsqrt(jnp.sum(widened * widened, axis=-1, keepdims=True) / width + EPSILON)
        out_ref[rows, pl.ds(0, width)] = (widened * scaling * gain_ref[...]).astype(BF16)
        table = jnp.zeros((row_count, LANES), F32)
        for k in range(top_count):
            chosen = ids_ref[0, step_at, :, k : k + 1]
            gate = gates_ref[0, step_at, :, k : k + 1]
            table = table + jnp.where(named == chosen, gate, 0.0)
        table = jnp.where(position < live_ref[:, step_at : step_at + 1], table, 0.0)
        high = table.astype(BF16).astype(F32)
        rest = table - high
        middle = rest.astype(BF16).astype(F32)
        low = rest - middle
        split = jnp.where(third == 0, high, jnp.where(third == 1, middle, low))
        split = jnp.where(lane < 3 * expert_count, split, 0.0)
        out_ref[rows, pl.ds(width, LANES)] = split.astype(BF16)


def make_payload(tokens, live_rows, expert_ids, gate_weights, norm_gain, expert_count):
    step_count, row_count, width = tokens.shape
    inputs = (live_rows, tokens, expert_ids, gate_weights, norm_gain)
    return pl.pallas_call(
        functools.partial(payload_kernel, expert_count),
        out_shape=jax.ShapeDtypeStruct((step_count * row_count, width + LANES), BF16),
        in_specs=[hbm_spec()] * 5,
        out_specs=vmem_spec(),
        scratch_shapes=[pltpu.VMEM(value.shape, value.dtype) for value in inputs] + [pltpu.SemaphoreType.DMA((5,))],
        compiler_params=small_grant(),
        cost_estimate=pl.CostEstimate(flops=8 * tokens.size, bytes_accessed=6 * tokens.size, transcendentals=0),
    )(*[in_hbm(value) for value in inputs])


def join_kernel(count, height, picks, masks, first_column, *refs):
    operands, outs = refs[:count], refs[len(refs) - len(picks) :]

    def total(block, columns):
        rows = pl.ds(block * height, height)
        value = operands[0][rows, columns].astype(F32)
        for operand in operands[1:]:
            value = value + operand[rows, columns].astype(F32)
        return value

    for blocks, out_ref in zip(picks, outs, strict=True):
        for at, block in enumerate(blocks):
            out_ref[pl.ds(at * height, height), :] = total(block, slice(None)).astype(out_ref.dtype)
    if not masks:
        return
    shared_ref = refs[count]
    features, width = shared_ref.shape[2], operands[0].shape[1]
    group = lax.div(lax.axis_index("expert"), 2)
    start = group * features - first_column

    @pl.when((start >= 0) & (start < width))
    def _():
        columns = pl.ds(pl.multiple_of(start, LANES), features)
        for blocks, out_ref in zip(picks, outs, strict=True):
            for at, block in enumerate(blocks):
                value = total(block, columns) + shared_ref[jnp.bitwise_xor(group, masks[block])].astype(F32)
                out_ref[pl.ds(at * height, height), columns] = value.astype(out_ref.dtype)


def join(operands, height, picks, shared=None, masks=(), first_column=0):
    columns = operands[0].shape[1]
    size = operands[0].size
    extra = [] if shared is None else [shared]
    return list(
        pl.pallas_call(
            functools.partial(
                join_kernel, len(operands), height, picks, () if shared is None else masks, first_column
            ),
            out_shape=[
                jax.ShapeDtypeStruct((len(blocks) * height, columns), F32 if at == 0 else BF16)
                for at, blocks in enumerate(picks)
            ],
            in_specs=[vmem_spec()] * (len(operands) + len(extra)),
            out_specs=[vmem_spec()] * len(picks),
            compiler_params=small_grant(),
            cost_estimate=pl.CostEstimate(
                flops=len(operands) * size, bytes_accessed=(2 * len(operands) + 4) * size, transcendentals=0
            ),
        )(*operands, *extra)
    )


def pair_copies(own_hbm, other_hbm, weight_ref, sems):
    features = own_hbm.shape[0]
    core = lax.rem(lax.axis_index("expert"), 2)
    own_at = pl.multiple_of(core * features, 16)
    other_at = pl.multiple_of((1 - core) * features, 16)
    own = pltpu.make_async_copy(own_hbm, weight_ref.at[pl.ds(own_at, features), :], sems.at[0])
    other = pltpu.make_async_copy(other_hbm, weight_ref.at[pl.ds(other_at, features), :], sems.at[1])
    return own, other


def shared_up_kernel(masks, *refs):
    blocks = refs[: len(masks)]
    own_hbm, other_hbm, out_ref, rows_ref, weight_ref, sems = refs[len(masks) :]
    height, width = blocks[0].shape
    features = weight_ref.shape[0]
    own, other = pair_copies(own_hbm, other_hbm, weight_ref, sems)
    own.start()
    other.start()
    group = lax.div(lax.axis_index("expert"), 2)
    start = 0 if width == features else pl.multiple_of(group * features, LANES)
    for at, block in enumerate(blocks):
        rows_ref[pl.ds(at * height, height), :] = block[:, pl.ds(start, features)]
    own.wait()
    other.wait()
    partial_value = jnp.dot(rows_ref[...], weight_ref[...], preferred_element_type=F32).astype(BF16)
    for at, mask in enumerate(masks):
        out_ref[jnp.bitwise_xor(group, mask)] = partial_value[at * height : (at + 1) * height]


def shared_up(blocks, masks, own, other):
    count, height = len(blocks), blocks[0].shape[0]
    features, columns = 2 * own.shape[0], own.shape[1]
    if features % LANES != 0:
        first = lax.axis_index("expert") // 2 * features
        blocks = [lax.dynamic_slice_in_dim(block, first, features, 1) for block in blocks]
    return pl.pallas_call(
        functools.partial(shared_up_kernel, masks),
        out_shape=jax.ShapeDtypeStruct((count, height, columns), BF16),
        in_specs=[vmem_spec()] * count + [any_spec()] * 2,
        out_specs=vmem_spec(),
        scratch_shapes=[
            pltpu.VMEM((count * height, features), BF16),
            pltpu.VMEM((features, columns), BF16),
            pltpu.SemaphoreType.DMA((2,)),
        ],
        compiler_params=small_grant(),
        cost_estimate=pl.CostEstimate(
            flops=2 * count * height * features * columns, bytes_accessed=2 * features * columns, transcendentals=0
        ),
    )(*blocks, in_hbm(own), other)


def shared_down_kernel(blocks_ref, own_hbm, other_hbm, out_ref, rows_ref, weight_ref, sems):
    count, height, _ = blocks_ref.shape
    own, other = pair_copies(own_hbm, other_hbm, weight_ref, sems)
    own.start()
    other.start()
    for at in range(count):
        rows_ref[pl.ds(at * height, height), :] = blocks_ref[at]
    own.wait()
    other.wait()
    contract = (((1,), (1,)), ((), ()))
    result = lax.dot_general(rows_ref[...], weight_ref[...], contract, preferred_element_type=F32).astype(BF16)
    for at in range(count):
        out_ref[at] = result[at * height : (at + 1) * height]


def shared_down_rows(blocks, own, other):
    count, height, depth = blocks.shape
    features = 2 * own.shape[0]
    return pl.pallas_call(
        shared_down_kernel,
        out_shape=jax.ShapeDtypeStruct((count, height, features), BF16),
        in_specs=[vmem_spec()] + [any_spec()] * 2,
        out_specs=vmem_spec(),
        scratch_shapes=[
            pltpu.VMEM((count * height, depth), BF16),
            pltpu.VMEM((features, depth), BF16),
            pltpu.SemaphoreType.DMA((2,)),
        ],
        compiler_params=small_grant(),
        cost_estimate=pl.CostEstimate(
            flops=2 * count * height * depth * features, bytes_accessed=2 * depth * features, transcendentals=0
        ),
    )(blocks, in_hbm(own), other)


def shared_hidden_kernel(parts_ref, out_ref):
    count, _, columns = parts_ref.shape
    total = parts_ref[0].astype(F32)
    for at in range(1, count):
        total = total + parts_ref[at].astype(F32)
    half = columns // 2
    hidden = (jax.nn.silu(total[:, :half]) * total[:, half:]).astype(BF16)
    for at in range(count):
        out_ref[at] = hidden


def shared_hidden(parts):
    count, height, columns = parts.shape
    return pl.pallas_call(
        shared_hidden_kernel,
        out_shape=jax.ShapeDtypeStruct((count, height, columns // 2), BF16),
        in_specs=[vmem_spec()],
        out_specs=vmem_spec(),
        compiler_params=small_grant(),
        cost_estimate=pl.CostEstimate(flops=parts.size, bytes_accessed=3 * parts.size, transcendentals=height * columns),
    )(parts)


def routed_up_kernel(block_count, expert_count, step, *refs):
    blocks = refs[:block_count]
    weight_hbm, hidden_ref, gate_ref, rows_ref, total_ref, near_ref, sems = refs[block_count:]
    height = blocks[0].shape[0]
    width, double = weight_hbm.shape
    units = double // 2
    count, slots = width // step, near_ref.shape[0]

    def fetch(at):
        slot = lax.rem(at, slots)
        rows = pl.ds(pl.multiple_of(at * step, step), step)
        return pltpu.make_async_copy(weight_hbm.at[rows, :], near_ref.at[slot], sems.at[slot])

    for at in range(min(slots, count)):
        fetch(jnp.int32(at)).start()

    expert = lax.div(lax.axis_index("expert"), lax.axis_size("expert") // expert_count)
    lane = lax.broadcasted_iota(jnp.int32, (height, LANES), 1)
    mine = (lane == expert) | (lane == expert + expert_count) | (lane == expert + 2 * expert_count)
    for at, block in enumerate(blocks):
        rows = pl.ds(at * height, height)
        rows_ref[rows, :] = block[:, pl.ds(0, width)]
        table = jnp.where(mine, block[:, pl.ds(width, LANES)].astype(F32), 0.0)
        gate_ref[rows, :] = jnp.broadcast_to(jnp.sum(table, axis=1, keepdims=True), (height, LANES))
    total_ref[...] = jnp.zeros_like(total_ref)

    def body(at, carry):
        fetch(at).wait()
        columns = pl.ds(pl.multiple_of(at * step, LANES), step)
        total_ref[...] += jnp.dot(rows_ref[:, columns], near_ref[lax.rem(at, slots)], preferred_element_type=F32)

        @pl.when(at + slots < count)
        def _():
            fetch(at + slots).start()

        return carry

    lax.fori_loop(0, count, body, 0)
    hidden_ref[...] = (jax.nn.silu(total_ref[:, :units]) * total_ref[:, units:]).astype(BF16)


def routed_up(blocks, weight, expert_count):
    height = blocks[0].shape[0]
    width, double = weight.shape
    rows = len(blocks) * height
    step = largest_step(width, 2 * LANES, UP_STEP)
    return pl.pallas_call(
        functools.partial(routed_up_kernel, len(blocks), expert_count, step),
        out_shape=[jax.ShapeDtypeStruct((rows, double // 2), BF16), jax.ShapeDtypeStruct((rows, LANES), F32)],
        in_specs=[vmem_spec()] * len(blocks) + [hbm_spec()],
        out_specs=[vmem_spec()] * 2,
        scratch_shapes=[
            pltpu.VMEM((rows, width), BF16),
            pltpu.VMEM((rows, double), F32),
            pltpu.VMEM((UP_SLOTS, step, double), BF16),
            pltpu.SemaphoreType.DMA((UP_SLOTS,)),
        ],
        compiler_params=pltpu.CompilerParams(vmem_limit_bytes=ROUTED_GRANT),
        cost_estimate=pl.CostEstimate(
            flops=2 * rows * width * double, bytes_accessed=2 * width * double, transcendentals=rows * double // 2
        ),
    )(*blocks, in_hbm(weight))


def routed_down_kernel(step, part_count, hidden_ref, gate_ref, weight_hbm, *refs):
    outs = refs[: 2 * part_count]
    near_ref, sems = refs[2 * part_count :]
    half_rows = hidden_ref.shape[0] // 2
    count, slots = weight_hbm.shape[1] // step, near_ref.shape[0]

    def fetch(at):
        slot = lax.rem(at, slots)
        columns = pl.ds(pl.multiple_of(at * step, LANES), step)
        return pltpu.make_async_copy(weight_hbm.at[:, columns], near_ref.at[slot], sems.at[slot])

    for at in range(min(slots, count)):
        fetch(jnp.int32(at)).start()
    gate = gate_ref[:, :1]
    first = 0
    for part in range(part_count):
        keep_ref, send_ref = outs[2 * part], outs[2 * part + 1]
        in_part = keep_ref.shape[1] // step

        def body(at, carry, first=first, keep_ref=keep_ref, send_ref=send_ref):
            whole_at = first + at
            fetch(whole_at).wait()
            result = jnp.dot(hidden_ref[...], near_ref[lax.rem(whole_at, slots)], preferred_element_type=F32)
            weighted = (result.astype(BF16).astype(F32) * gate).astype(BF16)
            columns = pl.ds(pl.multiple_of(at * step, LANES), step)
            keep_ref[:, columns] = weighted[:half_rows]
            send_ref[:, columns] = weighted[half_rows:]

            @pl.when(whole_at + slots < count)
            def _():
                fetch(whole_at + slots).start()

            return carry

        lax.fori_loop(0, in_part, body, 0)
        first += in_part


def routed_down(hidden, gate, weight, widths):
    rows, units = hidden.shape
    width = weight.shape[1]
    step = largest_step(math.gcd(*widths), LANES, DOWN_STEP)
    return pl.pallas_call(
        functools.partial(routed_down_kernel, step, len(widths)),
        out_shape=[jax.ShapeDtypeStruct((rows // 2, columns), BF16) for columns in widths for _ in range(2)],
        in_specs=[vmem_spec()] * 2 + [hbm_spec()],
        out_specs=[vmem_spec()] * (2 * len(widths)),
        scratch_shapes=[pltpu.VMEM((DOWN_SLOTS, units, step), BF16), pltpu.SemaphoreType.DMA((DOWN_SLOTS,))],
        compiler_params=pltpu.CompilerParams(vmem_limit_bytes=ROUTED_GRANT),
        cost_estimate=pl.CostEstimate(
            flops=2 * rows * width * units, bytes_accessed=2 * width * units, transcendentals=0
        ),
    )(hidden, gate, in_hbm(weight))


def finish_kernel(counts, live_ref, tokens_ref, *refs):
    out_ref = refs[-1]
    step_count, row_count, _ = tokens_ref.shape
    used, first = 0, 0
    for count in counts:
        total = refs[used][...]
        for at in range(1, count):
            total = total + refs[used + at][...].astype(F32)
        width = total.shape[1]
        position = lax.broadcasted_iota(jnp.int32, (row_count, width), 0)
        columns = pl.ds(first, width)
        for step_at in range(step_count):
            added = total[step_at * row_count : (step_at + 1) * row_count]
            masked = jnp.where(position < live_ref[:, step_at : step_at + 1], added, 0.0)
            out_ref[step_at, :, columns] = (tokens_ref[step_at, :, columns].astype(F32) + masked).astype(BF16)
        used += count
        first += width


def finish(tokens, live_rows, lines):
    flat = [line for group in lines for line in group]
    return pl.pallas_call(
        functools.partial(finish_kernel, [len(group) for group in lines]),
        out_shape=jax.ShapeDtypeStruct(tokens.shape, BF16),
        in_specs=[vmem_spec()] * (2 + len(flat)),
        out_specs=vmem_spec(),
        compiler_params=small_grant(),
        cost_estimate=pl.CostEstimate(flops=8 * tokens.size, bytes_accessed=12 * tokens.size, transcendentals=0),
    )(live_rows, tokens, *flat)


def per_device(
    tokens,
    live_rows,
    expert_ids,
    gate_weights,
    norm_gain,
    expert_gate_up,
    expert_down,
    shared_gate_up,
    shared_down,
):
    device_count = lax.axis_size("expert")
    line_count = device_count // 4
    height = tokens.shape[0] * tokens.shape[1]
    live = jnp.swapaxes(live_rows, 0, 1)

    def swap(value, mask):
        return lax.ppermute(value, "expert", [(i, i ^ mask) for i in range(device_count)])

    def swap_line(values):
        swapped = []
        for k, value in enumerate(values, 1):
            swapped.append(swap(value, 4 * k))
        return swapped

    groups = [[first + 2 * at for at in range(device_count // 2)] for first in range(2)]

    def exchange(value):
        return lax.all_to_all(value, "expert", 0, 0, axis_index_groups=groups, tiled=True)

    own_up, own_down = shared_gate_up[0], jnp.swapaxes(shared_down[0], 0, 1)
    other_up, other_down = swap(own_up, 1), swap(own_down, 1)
    payload = make_payload(tokens, live, expert_ids, gate_weights, norm_gain, EXPERTS)
    along = [payload] + swap_line([payload] * (line_count - 1))
    across = []
    for block in along:
        across.append(swap(block, 2))
    same = along + across
    masks = [2 * k for k in range(line_count)] + [2 * k + 1 for k in range(line_count)]
    beside = [swap(block, 1) for block in same]

    partial_value = shared_up(same, masks, own_up, other_up)
    width, features = tokens.shape[2], 2 * own_down.shape[0]
    unit = features if features % LANES == 0 else LANES
    first_width = (width // unit * FIRST_EIGHTHS + 4) // 8 * unit
    widths = [first_width, width - first_width]
    up_weight, down_weight = expert_gate_up[0, 0], expert_down[0, 0]
    up_weight, partial_value = lax.optimization_barrier((up_weight, partial_value))
    projected = exchange(partial_value)
    routed_hidden, gate = routed_up(same + beside, up_weight, EXPERTS)
    hidden = shared_hidden(projected)
    down_weight, hidden = lax.optimization_barrier((down_weight, hidden))
    spread = exchange(hidden)
    outs = routed_down(routed_hidden, gate, down_weight, widths)
    shared = shared_down_rows(spread, own_down, other_down)

    come = []
    for part in range(2):
        come.append(swap(outs[2 * part + 1], 1))
    lower, upper = list(range(line_count)), list(range(line_count, 2 * line_count))
    picks = ([lower, upper], [[k, line_count + k] for k in range(line_count)])
    joined = []
    for part in range(2):
        first = part * widths[0]
        if features % LANES == 0:
            joined.append(join([outs[2 * part], come[part]], height, picks[part], shared, masks, first))
        else:
            group = lax.axis_index("expert") // 2
            rows = shared[jnp.bitwise_xor(jnp.asarray(masks), group)].reshape(-1, features)
            wide = lax.dynamic_update_slice(
                jnp.zeros((rows.shape[0], width), BF16), rows, (0, group * features)
            )
            piece = wide[:, first : first + widths[part]]
            joined.append(join([outs[2 * part], come[part], piece], height, picks[part]))
    come_across = swap(joined[0][1], 2)
    come_along = swap_line(joined[1][1:])
    near = join([joined[0][0], come_across], height, [[k] for k in range(line_count)])
    first_lines = near[:1] + swap_line(near[1:])
    keep, send = join([joined[1][0]] + come_along, height, [[0], [1]])
    second_lines = [keep, swap(send, 2)]
    return finish(tokens, live, [first_lines, second_lines])


def solution(mesh):
    placed = (
        P(None, ("parts", "expert"), None),
        P(None, ("parts", "expert")),
        P(None, None, ("parts", "expert"), None),
        P(None, None, ("parts", "expert"), None),
        P(),
        P(None, "expert", None, None),
        P(None, "expert", None, None),
        P(None, "expert", None),
        P(None, None, "expert"),
    )
    return jax.shard_map(
        per_device,
        mesh=mesh,
        in_specs=placed,
        out_specs=P(None, ("parts", "expert"), None),
        check_vma=False,
    )
```

profile of v0, /device:TPU:0, one launch (start us, length us, event | category | flops | bytes accessed | tf_op | source)
XLA Modules:
  0.0 85.0 jit_solution(3369527906158088106)
XLA Ops:
  0.0 0.5 collective-permute-start.15
  0.5 1.2 %shard_map.91.refs_0_ = bf16[8,7296]{1,0:T(8,128)(2,1)S(1)} custom-call(s32[1,2]{1,0:T(1,128)} %bitcast.7, bf16[2,4,7168]{2,1,0:T(4,128)(2,1)} %tokens_ref.1, s32[1,2,4,8]{3,2,1,0:T(4,128)} %refs_2_.1, f32[1,2,4,8]{3,2,1,0:T(4,128)} %refs_3_.1, f32[1,7168]{1,0:T(1,128)} %refs_4_.1), custom_call_target="tpu_custom_call" | custom-call | flops 458752 | bytes 344064 | tf_op jit(solution)/shard_map/pallas_call | solution.py:92
  1.7 2.6 %collective-permute-start = (bf16[8,7296]{1,0:T(8,128)(2,1)S(1)}, bf16[8,7296]{1,0:T(8,128)(2,1)S(1)}, u32[]{:S(2)}, u32[]{:S(2)}) collective-permute-start(bf16[8,7296]{1,0:T(8,128)(2,1)S(1)} %shard_map.91.refs_0_), channel_id=1, source_target_pairs={{0,4},{1,5},{2,6},{3,7},{4,0},{5,1},{6,2},{7,3},{8,12},{9,13},{10,... | collective-permute-start | bytes 350216 | tf_op jit(solution)/shard_map/ppermute | solution.py:432
  4.3 2.6 %collective-permute-start.1 = (bf16[8,7296]{1,0:T(8,128)(2,1)S(1)}, bf16[8,7296]{1,0:T(8,128)(2,1)S(1)}, u32[]{:S(2)}, u32[]{:S(2)}) collective-permute-start(bf16[8,7296]{1,0:T(8,128)(2,1)S(1)} %shard_map.91.refs_0_), channel_id=1, source_target_pairs={{0,8},{1,9},{2,10},{3,11},{4,12},{5,13},{6,14},{7,15},{8,0},{9,1},... | collective-permute-start | bytes 350216 | tf_op jit(solution)/shard_map/ppermute | solution.py:432
  6.9 0.0 collective-permute-start.2
  6.9 1.7 %collective-permute-start.3 = (bf16[8,7296]{1,0:T(8,128)(2,1)S(1)}, bf16[8,7296]{1,0:T(8,128)(2,1)S(1)}, u32[]{:S(2)}, u32[]{:S(2)}) collective-permute-start(bf16[8,7296]{1,0:T(8,128)(2,1)S(1)} %shard_map.91.refs_0_), channel_id=1, source_target_pairs={{0,2},{1,3},{2,0},{3,1},{4,6},{5,7},{6,4},{7,5},{8,10},{9,11},{10,... | collective-permute-start | bytes 350216 | tf_op jit(solution)/shard_map/ppermute | solution.py:432
  8.6 1.3 %collective-permute-done.refs_1_ = bf16[8,7296]{1,0:T(8,128)(2,1)S(1)} collective-permute-done((bf16[8,7296]{1,0:T(8,128)(2,1)S(1)}, bf16[8,7296]{1,0:T(8,128)(2,1)S(1)}, u32[]{:S(2)}, u32[]{:S(2)}) %collective-permute-start) | collective-permute-done | bytes 116768 | tf_op jit(solution)/shard_map/ppermute | solution.py:432
  10.0 0.0 collective-permute-start.7
  10.0 6.3 %collective-permute-done.1.refs_2_ = bf16[8,7296]{1,0:T(8,128)(2,1)S(1)} collective-permute-done((bf16[8,7296]{1,0:T(8,128)(2,1)S(1)}, bf16[8,7296]{1,0:T(8,128)(2,1)S(1)}, u32[]{:S(2)}, u32[]{:S(2)}) %collective-permute-start.1) | collective-permute-done | bytes 116768 | tf_op jit(solution)/shard_map/ppermute | solution.py:432
  16.3 1.5 %collective-permute-start.4 = (bf16[8,7296]{1,0:T(8,128)(2,1)S(1)}, bf16[8,7296]{1,0:T(8,128)(2,1)S(1)}, u32[]{:S(2)}, u32[]{:S(2)}) collective-permute-start(bf16[8,7296]{1,0:T(8,128)(2,1)S(1)} %collective-permute-done.refs_1_), channel_id=1, source_target_pairs={{0,2},{1,3},{2,0},{3,1},{4,6},{5,7},{6,4},{7,5},{8,10},{9,11},{10,... | collective-permute-start | bytes 350216 | tf_op jit(solution)/shard_map/ppermute | solution.py:432
  17.8 0.0 collective-permute-done.2.refs_3_
  17.8 0.5 collective-permute-start.5
  18.3 0.0 collective-permute-done.3.refs_4_
  18.3 1.5 %collective-permute-start.6 = (bf16[8,7296]{1,0:T(8,128)(2,1)S(1)}, bf16[8,7296]{1,0:T(8,128)(2,1)S(1)}, u32[]{:S(2)}, u32[]{:S(2)}) collective-permute-start(bf16[8,7296]{1,0:T(8,128)(2,1)S(1)} %collective-permute-done.2.refs_3_), channel_id=1, source_target_pairs={{0,2},{1,3},{2,0},{3,1},{4,6},{5,7},{6,4},{7,5},{8,10},{9,11},{10,... | collective-permute-start | bytes 350216 | tf_op jit(solution)/shard_map/ppermute | solution.py:432
  19.9 0.0 collective-permute-done.7.refs_8_
  19.9 0.0 collective-permute-start.10
  19.9 1.5 %collective-permute-done.4.refs_5_ = bf16[8,7296]{1,0:T(8,128)(2,1)S(1)} collective-permute-done((bf16[8,7296]{1,0:T(8,128)(2,1)S(1)}, bf16[8,7296]{1,0:T(8,128)(2,1)S(1)}, u32[]{:S(2)}, u32[]{:S(2)}) %collective-permute-start.4) | collective-permute-done | bytes 116768 | tf_op jit(solution)/shard_map/ppermute | solution.py:432
  21.4 0.0 collective-permute-start.8
  21.4 1.2 %collective-permute-done.5.refs_6_ = bf16[8,7296]{1,0:T(8,128)(2,1)S(1)} collective-permute-done((bf16[8,7296]{1,0:T(8,128)(2,1)S(1)}, bf16[8,7296]{1,0:T(8,128)(2,1)S(1)}, u32[]{:S(2)}, u32[]{:S(2)}) %collective-permute-start.5) | collective-permute-done | bytes 116768 | tf_op jit(solution)/shard_map/ppermute | solution.py:432
  22.6 0.0 collective-permute-start.9
  22.6 1.2 %collective-permute-done.6.refs_7_ = bf16[8,7296]{1,0:T(8,128)(2,1)S(1)} collective-permute-done((bf16[8,7296]{1,0:T(8,128)(2,1)S(1)}, bf16[8,7296]{1,0:T(8,128)(2,1)S(1)}, u32[]{:S(2)}, u32[]{:S(2)}) %collective-permute-start.6) | collective-permute-done | bytes 116768 | tf_op jit(solution)/shard_map/ppermute | solution.py:432
  23.9 0.0 collective-permute-start.11
  23.9 0.0 collective-permute-done.10.refs_11_
  23.9 0.5 collective-permute-start.12
  24.4 0.1 collective-permute-start.13
  24.5 0.0 collective-permute-done.15.refs_9_
  24.5 0.4 collective-permute-start.14
  24.9 3.0 %shard_map.92 = bf16[8,8,2048]{2,1,0:T(8,128)(2,1)} custom-call(bf16[8,7296]{1,0:T(8,128)(2,1)S(1)} %shard_map.91.refs_0_, bf16[8,7296]{1,0:T(8,128)(2,1)S(1)} %collective-permute-done.refs_1_, bf16[8,7296]{1,0:T(8,128)(2,1)S(1)} %collective-permute-done.1.refs_2_, bf16[8,7296]{1,0:T(8,128)(2,1)S(1)} %collective-permute-done.2.refs_3_, ...), custom_call_target="tpu_custom_call" | custom-call | flops 234881024 | bytes 3670016 | tf_op jit(solution)/shard_map/pallas_call | solution.py:190
  27.9 5.9 %all-to-all-start = ((bf16[8,8,2048]{2,1,0:T(8,128)(2,1)}), bf16[8,8,2048]{2,1,0:T(8,128)(2,1)S(1)}, u32[]{:S(2)}, u32[]{:S(2)}) async-start(bf16[8,8,2048]{2,1,0:T(8,128)(2,1)} %shard_map.92), calls=%async_computation | async-start | bytes 524288 | tf_op jit(solution)/shard_map/all_to_all | solution.py:443
  33.8 0.1 collective-permute-start.17
  33.9 0.0 collective-permute-done.12.refs_13_
  33.9 0.0 collective-permute-done.13.refs_14_
  33.9 10.3 %shard_map.93 = (bf16[128,1024]{1,0:T(8,128)(2,1)S(1)}, f32[128,128]{1,0:T(8,128)S(1)}) custom-call(bf16[8,7296]{1,0:T(8,128)(2,1)S(1)} %shard_map.91.refs_0_, bf16[8,7296]{1,0:T(8,128)(2,1)S(1)} %collective-permute-done.refs_1_, bf16[8,7296]{1,0:T(8,128)(2,1)S(1)} %collective-permute-done.1.refs_2_, bf16[8,7296]{1,0:T(8,128)(2,1)S(1)} %collective-permute-done.2.refs_3_, ...), custom_call_target="tpu_custom_call" | custom-call | flops 3758096384 | bytes 29360128 | tf_op jit(solution)/shard_map/pallas_call | solution.py:311
  44.2 0.0 copy-start
  44.2 0.0 copy-start.1
  44.2 0.0 all-to-all-done.parts_ref
  44.2 0.7 shard_map.94
  44.9 6.6 %shard_map.95 = (bf16[64,4480]{1,0:T(8,128)(2,1)S(1)}, bf16[64,4480]{1,0:T(8,128)(2,1)}, bf16[64,2688]{1,0:T(8,128)(2,1)S(1)}, bf16[64,2688]{1,0:T(8,128)(2,1)S(1)}) custom-call(bf16[128,1024]{1,0:T(8,128)(2,1)S(1)} %get-tuple-element.28.hidden_ref, f32[128,128]{1,0:T(8,128)S(1)} %get-tuple-element.29.gate_ref, bf16[1024,7168]{1,0:T(8,128)(2,1)} %bitcast.10), custom_call_target="tpu_custom_call" | custom-call | flops 1879048192 | bytes 14680064 | tf_op jit(solution)/shard_map/pallas_call | solution.py:371
  51.5 0.8 copy-done.2
  52.3 0.5 collective-permute-start.16
  52.8 5.9 %all-to-all-start.1 = ((bf16[8,8,1024]{2,1,0:T(8,128)(2,1)}), bf16[8,8,1024]{2,1,0:T(8,128)(2,1)S(1)}, u32[]{:S(2)}, u32[]{:S(2)}) async-start(bf16[8,8,1024]{2,1,0:T(8,128)(2,1)} %shard_map.94), calls=%async_computation.1 | async-start | bytes 262144 | tf_op jit(solution)/shard_map/all_to_all | solution.py:443
  58.7 7.3 %all-to-all-done.1.blocks_ref = bf16[8,8,1024]{2,1,0:T(8,128)(2,1)S(1)} async-done(((bf16[8,8,1024]{2,1,0:T(8,128)(2,1)}), bf16[8,8,1024]{2,1,0:T(8,128)(2,1)S(1)}, u32[]{:S(2)}, u32[]{:S(2)}) %all-to-all-start.1) | async-done | bytes 131104 | tf_op jit(solution)/shard_map/all_to_all | solution.py:443
  66.0 1.9 %shard_map.96.refs_2_ = bf16[8,8,896]{2,1,0:T(8,128)(2,1)S(1)} custom-call(bf16[8,8,1024]{2,1,0:T(8,128)(2,1)S(1)} %all-to-all-done.1.blocks_ref, bf16[448,1024]{1,0:T(8,128)(2,1)} %bitcast.14, bf16[448,1024]{1,0:T(8,128)(2,1)S(1)} %collective-permute-done.17.other_hbm), custom_call_target="tpu_custom_call" | custom-call | flops 117440512 | bytes 1835008 | tf_op jit(solution)/shard_map/pallas_call | solution.py:225
  67.9 0.2 shard_map.97
  68.1 0.4 collective-permute-start.18
  68.5 0.0 collective-permute-done.22.refs_1_
  68.5 0.1 shard_map.99
  68.6 1.0 %collective-permute-start.23 = (bf16[16,2688]{1,0:T(8,128)(2,1)S(1)}, bf16[16,2688]{1,0:T(8,128)(2,1)S(1)}, u32[]{:S(2)}, u32[]{:S(2)}) collective-permute-start(bf16[16,2688]{1,0:T(8,128)(2,1)S(1)} %get-tuple-element.44), channel_id=1, source_target_pairs={{0,4},{1,5},{2,6},{3,7},{4,0},{5,1},{6,2},{7,3},{8,12},{9,13},{10,... | collective-permute-start | bytes 258056 | tf_op jit(solution)/shard_map/ppermute | solution.py:432
  69.6 1.1 %collective-permute-start.24 = (bf16[16,2688]{1,0:T(8,128)(2,1)S(1)}, bf16[16,2688]{1,0:T(8,128)(2,1)S(1)}, u32[]{:S(2)}, u32[]{:S(2)}) collective-permute-start(bf16[16,2688]{1,0:T(8,128)(2,1)S(1)} %get-tuple-element.45), channel_id=1, source_target_pairs={{0,8},{1,9},{2,10},{3,11},{4,12},{5,13},{6,14},{7,15},{8,0},{9,1},... | collective-permute-start | bytes 258056 | tf_op jit(solution)/shard_map/ppermute | solution.py:432
  70.7 2.4 %collective-permute-start.25 = (bf16[16,2688]{1,0:T(8,128)(2,1)S(1)}, bf16[16,2688]{1,0:T(8,128)(2,1)S(1)}, u32[]{:S(2)}, u32[]{:S(2)}) collective-permute-start(bf16[16,2688]{1,0:T(8,128)(2,1)S(1)} %get-tuple-element.46), channel_id=1, source_target_pairs={{0,12},{1,13},{2,14},{3,15},{4,8},{5,9},{6,10},{7,11},{8,4},{9,5},... | collective-permute-start | bytes 258056 | tf_op jit(solution)/shard_map/ppermute | solution.py:432
  73.1 2.4 %collective-permute-done.18.refs_1_ = bf16[32,4480]{1,0:T(8,128)(2,1)S(1)} collective-permute-done((bf16[32,4480]{1,0:T(8,128)(2,1)S(1)}, bf16[32,4480]{1,0:T(8,128)(2,1)S(1)}, u32[]{:S(2)}, u32[]{:S(2)}) %collective-permute-start.18) | collective-permute-done | bytes 286752 | tf_op jit(solution)/shard_map/ppermute | solution.py:432
  75.5 0.1 shard_map.98
  75.6 0.2 collective-permute-start.19
  75.8 1.7 %collective-permute-start.20 = (bf16[8,4480]{1,0:T(8,128)(2,1)S(1)}, bf16[8,4480]{1,0:T(8,128)(2,1)S(1)}, u32[]{:S(2)}, u32[]{:S(2)}) collective-permute-start(bf16[8,4480]{1,0:T(8,128)(2,1)S(1)} %get-tuple-element.39), channel_id=1, source_target_pairs={{0,8},{1,9},{2,10},{3,11},{4,12},{5,13},{6,14},{7,15},{8,0},{9,1},... | collective-permute-start | bytes 215048 | tf_op jit(solution)/shard_map/ppermute | solution.py:432
  77.4 0.0 collective-permute-done.23.refs_1_
  77.4 2.6 %collective-permute-start.21 = (bf16[8,4480]{1,0:T(8,128)(2,1)S(1)}, bf16[8,4480]{1,0:T(8,128)(2,1)S(1)}, u32[]{:S(2)}, u32[]{:S(2)}) collective-permute-start(bf16[8,4480]{1,0:T(8,128)(2,1)S(1)} %get-tuple-element.40), channel_id=1, source_target_pairs={{0,12},{1,13},{2,14},{3,15},{4,8},{5,9},{6,10},{7,11},{8,4},{9,5},... | collective-permute-start | bytes 215048 | tf_op jit(solution)/shard_map/ppermute | solution.py:432
  80.0 0.0 collective-permute-done.24.refs_2_
  80.0 0.0 collective-permute-done.25.refs_3_
  80.1 0.4 collective-permute-start.26
  80.5 3.7 %collective-permute-done.26.refs_5_ = bf16[8,2688]{1,0:T(8,128)(2,1)S(1)} collective-permute-done((bf16[8,2688]{1,0:T(8,128)(2,1)S(1)}, bf16[8,2688]{1,0:T(8,128)(2,1)S(1)}, u32[]{:S(2)}, u32[]{:S(2)}) %collective-permute-start.26) | collective-permute-done | bytes 43040 | tf_op jit(solution)/shard_map/ppermute | solution.py:432
  84.2 0.0 collective-permute-done.19.refs_1_
  84.2 0.0 collective-permute-done.20.refs_2_
  84.2 0.0 collective-permute-done.21.refs_3_
  84.2 0.8 shard_map.101
  (11 shorter events, 0.1 us)
Async XLA Ops:
  0.0 24.5 %collective-permute-start.15 = (bf16[448,2048]{1,0:T(8,128)(2,1)}, bf16[448,2048]{1,0:T(8,128)(2,1)S(1)}, u32[]{:S(2)}, u32[]{:S(2)}) collective-permute-start(bf16[448,2048]{1,0:T(8,128)(2,1)} %bitcast.11), channel_id=1, source_target_pairs={{0,1},{1,0},{2,3},{3,2},{4,5},{5,4},{6,7},{7,6},{8,9},{9,8},{10,11... | collective-permute-start | bytes 5505032 | tf_op jit(solution)/shard_map/ppermute | solution.py:432
  1.7 8.3 %collective-permute-start = (bf16[8,7296]{1,0:T(8,128)(2,1)S(1)}, bf16[8,7296]{1,0:T(8,128)(2,1)S(1)}, u32[]{:S(2)}, u32[]{:S(2)}) collective-permute-start(bf16[8,7296]{1,0:T(8,128)(2,1)S(1)} %shard_map.91.refs_0_), channel_id=1, source_target_pairs={{0,4},{1,5},{2,6},{3,7},{4,0},{5,1},{6,2},{7,3},{8,12},{9,13},{10,... | collective-permute-start | bytes 350216 | tf_op jit(solution)/shard_map/ppermute | solution.py:432
  4.3 12.0 %collective-permute-start.1 = (bf16[8,7296]{1,0:T(8,128)(2,1)S(1)}, bf16[8,7296]{1,0:T(8,128)(2,1)S(1)}, u32[]{:S(2)}, u32[]{:S(2)}) collective-permute-start(bf16[8,7296]{1,0:T(8,128)(2,1)S(1)} %shard_map.91.refs_0_), channel_id=1, source_target_pairs={{0,8},{1,9},{2,10},{3,11},{4,12},{5,13},{6,14},{7,15},{8,0},{9,1},... | collective-permute-start | bytes 350216 | tf_op jit(solution)/shard_map/ppermute | solution.py:432
  6.9 10.9 %collective-permute-start.2 = (bf16[8,7296]{1,0:T(8,128)(2,1)S(1)}, bf16[8,7296]{1,0:T(8,128)(2,1)S(1)}, u32[]{:S(2)}, u32[]{:S(2)}) collective-permute-start(bf16[8,7296]{1,0:T(8,128)(2,1)S(1)} %shard_map.91.refs_0_), channel_id=1, source_target_pairs={{0,12},{1,13},{2,14},{3,15},{4,8},{5,9},{6,10},{7,11},{8,4},{9,5},... | collective-permute-start | bytes 350216 | tf_op jit(solution)/shard_map/ppermute | solution.py:432
  6.9 11.5 %collective-permute-start.3 = (bf16[8,7296]{1,0:T(8,128)(2,1)S(1)}, bf16[8,7296]{1,0:T(8,128)(2,1)S(1)}, u32[]{:S(2)}, u32[]{:S(2)}) collective-permute-start(bf16[8,7296]{1,0:T(8,128)(2,1)S(1)} %shard_map.91.refs_0_), channel_id=1, source_target_pairs={{0,2},{1,3},{2,0},{3,1},{4,6},{5,7},{6,4},{7,5},{8,10},{9,11},{10,... | collective-permute-start | bytes 350216 | tf_op jit(solution)/shard_map/ppermute | solution.py:432
  10.0 9.9 %collective-permute-start.7 = (bf16[8,7296]{1,0:T(8,128)(2,1)S(1)}, bf16[8,7296]{1,0:T(8,128)(2,1)S(1)}, u32[]{:S(2)}, u32[]{:S(2)}) collective-permute-start(bf16[8,7296]{1,0:T(8,128)(2,1)S(1)} %shard_map.91.refs_0_), channel_id=1, source_target_pairs={{0,1},{1,0},{2,3},{3,2},{4,5},{5,4},{6,7},{7,6},{8,9},{9,8},{10,11... | collective-permute-start | bytes 350216 | tf_op jit(solution)/shard_map/ppermute | solution.py:432
  16.3 5.1 %collective-permute-start.4 = (bf16[8,7296]{1,0:T(8,128)(2,1)S(1)}, bf16[8,7296]{1,0:T(8,128)(2,1)S(1)}, u32[]{:S(2)}, u32[]{:S(2)}) collective-permute-start(bf16[8,7296]{1,0:T(8,128)(2,1)S(1)} %collective-permute-done.refs_1_), channel_id=1, source_target_pairs={{0,2},{1,3},{2,0},{3,1},{4,6},{5,7},{6,4},{7,5},{8,10},{9,11},{10,... | collective-permute-start | bytes 350216 | tf_op jit(solution)/shard_map/ppermute | solution.py:432
  17.8 4.8 %collective-permute-start.5 = (bf16[8,7296]{1,0:T(8,128)(2,1)S(1)}, bf16[8,7296]{1,0:T(8,128)(2,1)S(1)}, u32[]{:S(2)}, u32[]{:S(2)}) collective-permute-start(bf16[8,7296]{1,0:T(8,128)(2,1)S(1)} %collective-permute-done.1.refs_2_), channel_id=1, source_target_pairs={{0,2},{1,3},{2,0},{3,1},{4,6},{5,7},{6,4},{7,5},{8,10},{9,11},{10,... | collective-permute-start | bytes 350216 | tf_op jit(solution)/shard_map/ppermute | solution.py:432
  18.3 5.6 %collective-permute-start.6 = (bf16[8,7296]{1,0:T(8,128)(2,1)S(1)}, bf16[8,7296]{1,0:T(8,128)(2,1)S(1)}, u32[]{:S(2)}, u32[]{:S(2)}) collective-permute-start(bf16[8,7296]{1,0:T(8,128)(2,1)S(1)} %collective-permute-done.2.refs_3_), channel_id=1, source_target_pairs={{0,2},{1,3},{2,0},{3,1},{4,6},{5,7},{6,4},{7,5},{8,10},{9,11},{10,... | collective-permute-start | bytes 350216 | tf_op jit(solution)/shard_map/ppermute | solution.py:432
  19.9 4.0 %collective-permute-start.10 = (bf16[8,7296]{1,0:T(8,128)(2,1)S(1)}, bf16[8,7296]{1,0:T(8,128)(2,1)S(1)}, u32[]{:S(2)}, u32[]{:S(2)}) collective-permute-start(bf16[8,7296]{1,0:T(8,128)(2,1)S(1)} %collective-permute-done.2.refs_3_), channel_id=1, source_target_pairs={{0,1},{1,0},{2,3},{3,2},{4,5},{5,4},{6,7},{7,6},{8,9},{9,8},{10,11... | collective-permute-start | bytes 350216 | tf_op jit(solution)/shard_map/ppermute | solution.py:432
  21.4 3.0 %collective-permute-start.8 = (bf16[8,7296]{1,0:T(8,128)(2,1)S(1)}, bf16[8,7296]{1,0:T(8,128)(2,1)S(1)}, u32[]{:S(2)}, u32[]{:S(2)}) collective-permute-start(bf16[8,7296]{1,0:T(8,128)(2,1)S(1)} %collective-permute-done.refs_1_), channel_id=1, source_target_pairs={{0,1},{1,0},{2,3},{3,2},{4,5},{5,4},{6,7},{7,6},{8,9},{9,8},{10,11... | collective-permute-start | bytes 350216 | tf_op jit(solution)/shard_map/ppermute | solution.py:432
  22.6 11.1 %collective-permute-start.9 = (bf16[8,7296]{1,0:T(8,128)(2,1)S(1)}, bf16[8,7296]{1,0:T(8,128)(2,1)S(1)}, u32[]{:S(2)}, u32[]{:S(2)}) collective-permute-start(bf16[8,7296]{1,0:T(8,128)(2,1)S(1)} %collective-permute-done.1.refs_2_), channel_id=1, source_target_pairs={{0,1},{1,0},{2,3},{3,2},{4,5},{5,4},{6,7},{7,6},{8,9},{9,8},{10,11... | collective-permute-start | bytes 350216 | tf_op jit(solution)/shard_map/ppermute | solution.py:432
  23.9 10.0 %collective-permute-start.11 = (bf16[8,7296]{1,0:T(8,128)(2,1)S(1)}, bf16[8,7296]{1,0:T(8,128)(2,1)S(1)}, u32[]{:S(2)}, u32[]{:S(2)}) collective-permute-start(bf16[8,7296]{1,0:T(8,128)(2,1)S(1)} %collective-permute-done.3.refs_4_), channel_id=1, source_target_pairs={{0,1},{1,0},{2,3},{3,2},{4,5},{5,4},{6,7},{7,6},{8,9},{9,8},{10,11... | collective-permute-start | bytes 350216 | tf_op jit(solution)/shard_map/ppermute | solution.py:432
  23.9 10.0 %collective-permute-start.12 = (bf16[8,7296]{1,0:T(8,128)(2,1)S(1)}, bf16[8,7296]{1,0:T(8,128)(2,1)S(1)}, u32[]{:S(2)}, u32[]{:S(2)}) collective-permute-start(bf16[8,7296]{1,0:T(8,128)(2,1)S(1)} %collective-permute-done.4.refs_5_), channel_id=1, source_target_pairs={{0,1},{1,0},{2,3},{3,2},{4,5},{5,4},{6,7},{7,6},{8,9},{9,8},{10,11... | collective-permute-start | bytes 350216 | tf_op jit(solution)/shard_map/ppermute | solution.py:432
  24.4 9.5 %collective-permute-start.13 = (bf16[8,7296]{1,0:T(8,128)(2,1)S(1)}, bf16[8,7296]{1,0:T(8,128)(2,1)S(1)}, u32[]{:S(2)}, u32[]{:S(2)}) collective-permute-start(bf16[8,7296]{1,0:T(8,128)(2,1)S(1)} %collective-permute-done.5.refs_6_), channel_id=1, source_target_pairs={{0,1},{1,0},{2,3},{3,2},{4,5},{5,4},{6,7},{7,6},{8,9},{9,8},{10,11... | collective-permute-start | bytes 350216 | tf_op jit(solution)/shard_map/ppermute | solution.py:432
  24.5 9.4 %collective-permute-start.14 = (bf16[8,7296]{1,0:T(8,128)(2,1)S(1)}, bf16[8,7296]{1,0:T(8,128)(2,1)S(1)}, u32[]{:S(2)}, u32[]{:S(2)}) collective-permute-start(bf16[8,7296]{1,0:T(8,128)(2,1)S(1)} %collective-permute-done.6.refs_7_), channel_id=1, source_target_pairs={{0,1},{1,0},{2,3},{3,2},{4,5},{5,4},{6,7},{7,6},{8,9},{9,8},{10,11... | collective-permute-start | bytes 350216 | tf_op jit(solution)/shard_map/ppermute | solution.py:432
  27.9 16.3 %all-to-all-start = ((bf16[8,8,2048]{2,1,0:T(8,128)(2,1)}), bf16[8,8,2048]{2,1,0:T(8,128)(2,1)S(1)}, u32[]{:S(2)}, u32[]{:S(2)}) async-start(bf16[8,8,2048]{2,1,0:T(8,128)(2,1)} %shard_map.92), calls=%async_computation | async-start | bytes 524288 | tf_op jit(solution)/shard_map/all_to_all | solution.py:443
  33.8 24.9 %collective-permute-start.17 = (bf16[448,1024]{1,0:T(8,128)(2,1)}, bf16[448,1024]{1,0:T(8,128)(2,1)S(1)}, u32[]{:S(2)}, u32[]{:S(2)}) collective-permute-start(bf16[448,1024]{1,0:T(8,128)(2,1)} %bitcast.13), channel_id=1, source_target_pairs={{0,1},{1,0},{2,3},{3,2},{4,5},{5,4},{6,7},{7,6},{8,9},{9,8},{10,11... | collective-permute-start | bytes 2752520 | tf_op jit(solution)/shard_map/ppermute | solution.py:432
  44.2 40.0 %copy-start = (bf16[2,4,7168]{2,1,0:T(4,128)(2,1)S(1)}, bf16[2,4,7168]{2,1,0:T(4,128)(2,1)}, u32[]{:S(2)}) copy-start(bf16[2,4,7168]{2,1,0:T(4,128)(2,1)} %tokens_ref.1) | copy-start | bytes 344068
  44.2 40.0 %copy-start.1 = (s32[2,1]{0,1:T(1,128)S(1)}, s32[2,1]{0,1:T(1,128)}, u32[]{:S(2)}) copy-start(s32[2,1]{0,1:T(1,128)} %param.10) | copy-start | bytes 28
  51.5 0.8 copy-start.2
  52.3 15.6 %collective-permute-start.16 = (bf16[64,4480]{1,0:T(8,128)(2,1)}, bf16[64,4480]{1,0:T(8,128)(2,1)S(1)}, u32[]{:S(2)}, u32[]{:S(2)}) collective-permute-start(bf16[64,4480]{1,0:T(8,128)(2,1)} %get-tuple-element.33), channel_id=1, source_target_pairs={{0,1},{1,0},{2,3},{3,2},{4,5},{5,4},{6,7},{7,6},{8,9},{9,8},{10,11... | collective-permute-start | bytes 1720328 | tf_op jit(solution)/shard_map/ppermute | solution.py:432
  52.8 13.3 %all-to-all-start.1 = ((bf16[8,8,1024]{2,1,0:T(8,128)(2,1)}), bf16[8,8,1024]{2,1,0:T(8,128)(2,1)S(1)}, u32[]{:S(2)}, u32[]{:S(2)}) async-start(bf16[8,8,1024]{2,1,0:T(8,128)(2,1)} %shard_map.94), calls=%async_computation.1 | async-start | bytes 262144 | tf_op jit(solution)/shard_map/all_to_all | solution.py:443
  58.7 9.8 %collective-permute-start.22 = (bf16[64,2688]{1,0:T(8,128)(2,1)}, bf16[64,2688]{1,0:T(8,128)(2,1)S(1)}, u32[]{:S(2)}, u32[]{:S(2)}) collective-permute-start(bf16[64,2688]{1,0:T(8,128)(2,1)} %copy-done.2), channel_id=1, source_target_pairs={{0,1},{1,0},{2,3},{3,2},{4,5},{5,4},{6,7},{7,6},{8,9},{9,8},{10,11... | collective-permute-start | bytes 1032200 | tf_op jit(solution)/shard_map/ppermute | solution.py:432
  68.1 7.4 %collective-permute-start.18 = (bf16[32,4480]{1,0:T(8,128)(2,1)S(1)}, bf16[32,4480]{1,0:T(8,128)(2,1)S(1)}, u32[]{:S(2)}, u32[]{:S(2)}) collective-permute-start(bf16[32,4480]{1,0:T(8,128)(2,1)S(1)} %get-tuple-element.36), channel_id=1, source_target_pairs={{0,2},{1,3},{2,0},{3,1},{4,6},{5,7},{6,4},{7,5},{8,10},{9,11},{10,... | collective-permute-start | bytes 860168 | tf_op jit(solution)/shard_map/ppermute | solution.py:432
  68.6 8.8 %collective-permute-start.23 = (bf16[16,2688]{1,0:T(8,128)(2,1)S(1)}, bf16[16,2688]{1,0:T(8,128)(2,1)S(1)}, u32[]{:S(2)}, u32[]{:S(2)}) collective-permute-start(bf16[16,2688]{1,0:T(8,128)(2,1)S(1)} %get-tuple-element.44), channel_id=1, source_target_pairs={{0,4},{1,5},{2,6},{3,7},{4,0},{5,1},{6,2},{7,3},{8,12},{9,13},{10,... | collective-permute-start | bytes 258056 | tf_op jit(solution)/shard_map/ppermute | solution.py:432
  69.6 10.4 %collective-permute-start.24 = (bf16[16,2688]{1,0:T(8,128)(2,1)S(1)}, bf16[16,2688]{1,0:T(8,128)(2,1)S(1)}, u32[]{:S(2)}, u32[]{:S(2)}) collective-permute-start(bf16[16,2688]{1,0:T(8,128)(2,1)S(1)} %get-tuple-element.45), channel_id=1, source_target_pairs={{0,8},{1,9},{2,10},{3,11},{4,12},{5,13},{6,14},{7,15},{8,0},{9,1},... | collective-permute-start | bytes 258056 | tf_op jit(solution)/shard_map/ppermute | solution.py:432
  70.7 9.3 %collective-permute-start.25 = (bf16[16,2688]{1,0:T(8,128)(2,1)S(1)}, bf16[16,2688]{1,0:T(8,128)(2,1)S(1)}, u32[]{:S(2)}, u32[]{:S(2)}) collective-permute-start(bf16[16,2688]{1,0:T(8,128)(2,1)S(1)} %get-tuple-element.46), channel_id=1, source_target_pairs={{0,12},{1,13},{2,14},{3,15},{4,8},{5,9},{6,10},{7,11},{8,4},{9,5},... | collective-permute-start | bytes 258056 | tf_op jit(solution)/shard_map/ppermute | solution.py:432
  75.6 8.6 %collective-permute-start.19 = (bf16[8,4480]{1,0:T(8,128)(2,1)S(1)}, bf16[8,4480]{1,0:T(8,128)(2,1)S(1)}, u32[]{:S(2)}, u32[]{:S(2)}) collective-permute-start(bf16[8,4480]{1,0:T(8,128)(2,1)S(1)} %get-tuple-element.38), channel_id=1, source_target_pairs={{0,4},{1,5},{2,6},{3,7},{4,0},{5,1},{6,2},{7,3},{8,12},{9,13},{10,... | collective-permute-start | bytes 215048 | tf_op jit(solution)/shard_map/ppermute | solution.py:432
  75.8 8.4 %collective-permute-start.20 = (bf16[8,4480]{1,0:T(8,128)(2,1)S(1)}, bf16[8,4480]{1,0:T(8,128)(2,1)S(1)}, u32[]{:S(2)}, u32[]{:S(2)}) collective-permute-start(bf16[8,4480]{1,0:T(8,128)(2,1)S(1)} %get-tuple-element.39), channel_id=1, source_target_pairs={{0,8},{1,9},{2,10},{3,11},{4,12},{5,13},{6,14},{7,15},{8,0},{9,1},... | collective-permute-start | bytes 215048 | tf_op jit(solution)/shard_map/ppermute | solution.py:432
  77.4 6.7 %collective-permute-start.21 = (bf16[8,4480]{1,0:T(8,128)(2,1)S(1)}, bf16[8,4480]{1,0:T(8,128)(2,1)S(1)}, u32[]{:S(2)}, u32[]{:S(2)}) collective-permute-start(bf16[8,4480]{1,0:T(8,128)(2,1)S(1)} %get-tuple-element.40), channel_id=1, source_target_pairs={{0,12},{1,13},{2,14},{3,15},{4,8},{5,9},{6,10},{7,11},{8,4},{9,5},... | collective-permute-start | bytes 215048 | tf_op jit(solution)/shard_map/ppermute | solution.py:432
  80.1 4.1 %collective-permute-start.26 = (bf16[8,2688]{1,0:T(8,128)(2,1)S(1)}, bf16[8,2688]{1,0:T(8,128)(2,1)S(1)}, u32[]{:S(2)}, u32[]{:S(2)}) collective-permute-start(bf16[8,2688]{1,0:T(8,128)(2,1)S(1)} %get-tuple-element.48), channel_id=1, source_target_pairs={{0,2},{1,3},{2,0},{3,1},{4,6},{5,7},{6,4},{7,5},{8,10},{9,11},{10,... | collective-permute-start | bytes 129032 | tf_op jit(solution)/shard_map/ppermute | solution.py:432
where the time goes:
time: 85.4 us; the launch traced here: 85 us
  starting transfers between devices  34.1 us (40%)
  waiting for transfers between devices  25.2 us (30%)
  Pallas kernels  24.7 us (29%)
    ppermute x27, starting transfers between devices, swap(): lax.ppermute(value, 'expert', [(i, i ^ mask) for i in range(device_count)])  22.3 us
    ppermute x27, waiting for transfers between devices, swap(): lax.ppermute(value, 'expert', [(i, i ^ mask) for i in range(device_count)])  17.9 us
    all_to_all x2, starting transfers between devices, exchange(): lax.all_to_all(value, 'expert', 0, 0, axis_index_groups=groups, tiled=True)  11.8 us
    pallas_call x1, Pallas kernels, routed_up(): pl.pallas_call(functools.partial(routed_up_kernel, len(blocks), expert_co...  10.3 us
    all_to_all x2, waiting for transfers between devices, exchange(): lax.all_to_all(value, 'expert', 0, 0, axis_index_groups=groups, tiled=True)  7.33 us
    pallas_call x1, Pallas kernels, routed_down(): pl.pallas_call(functools.partial(routed_down_kernel, step, len(widths)),...  6.6 us
    pallas_call x1, Pallas kernels, shared_up(): pl.pallas_call(functools.partial(shared_up_kernel, masks), out_shape=jax....  2.97 us
    pallas_call x1, Pallas kernels, shared_down_rows(): pl.pallas_call(shared_down_kernel, out_shape=jax.ShapeDtypeStruct((count,...  1.87 us
  transfers between devices with their start and end apart: 29, of which 8 were waited for; matrix products, arithmetic and copies ran while one was open for 0% of the time, Pallas kernels for 28%

commit v1 on v0

--- a/solution.py
+++ b/solution.py
@@ -162,46 +162,58 @@
     return own, other
 
 
+def pair_kernel(own_hbm, other_hbm, weight_ref, sems):
+    copies = pair_copies(own_hbm, other_hbm, weight_ref, sems)
+    for copy in copies:
+        copy.start()
+    for copy in copies:
+        copy.wait()
+
+
+def pair_up(own, other):
+    rows, columns = own.shape
+    return pl.pallas_call(
+        pair_kernel,
+        out_shape=pltpu.VMEM((2 * rows, columns), BF16),
+        in_specs=[any_spec()] * 2,
+        out_specs=vmem_spec(),
+        scratch_shapes=[pltpu.SemaphoreType.DMA((2,))],
+        compiler_params=small_grant(),
+        cost_estimate=pl.CostEstimate(flops=0, bytes_accessed=4 * rows * columns, transcendentals=0),
+    )(in_hbm(own), other)
+
+
 def shared_up_kernel(masks, *refs):
     blocks = refs[: len(masks)]
-    own_hbm, other_hbm, out_ref, rows_ref, weight_ref, sems = refs[len(masks) :]
+    weight_ref, out_ref, rows_ref = refs[len(masks) :]
     height, width = blocks[0].shape
     features = weight_ref.shape[0]
-    own, other = pair_copies(own_hbm, other_hbm, weight_ref, sems)
-    own.start()
-    other.start()
     group = lax.div(lax.axis_index("expert"), 2)
     start = 0 if width == features else pl.multiple_of(group * features, LANES)
     for at, block in enumerate(blocks):
         rows_ref[pl.ds(at * height, height), :] = block[:, pl.ds(start, features)]
-    own.wait()
-    other.wait()
     partial_value = jnp.dot(rows_ref[...], weight_ref[...], preferred_element_type=F32).astype(BF16)
     for at, mask in enumerate(masks):
         out_ref[jnp.bitwise_xor(group, mask)] = partial_value[at * height : (at + 1) * height]
 
 
-def shared_up(blocks, masks, own, other):
+def shared_up(blocks, masks, weight):
     count, height = len(blocks), blocks[0].shape[0]
-    features, columns = 2 * own.shape[0], own.shape[1]
+    features, columns = weight.shape
     if features % LANES != 0:
         first = lax.axis_index("expert") // 2 * features
         blocks = [lax.dynamic_slice_in_dim(block, first, features, 1) for block in blocks]
     return pl.pallas_call(
         functools.partial(shared_up_kernel, masks),
         out_shape=jax.ShapeDtypeStruct((count, height, columns), BF16),
-        in_specs=[vmem_spec()] * count + [any_spec()] * 2,
+        in_specs=[vmem_spec()] * (count + 1),
         out_specs=vmem_spec(),
-        scratch_shapes=[
-            pltpu.VMEM((count * height, features), BF16),
-            pltpu.VMEM((features, columns), BF16),
-            pltpu.SemaphoreType.DMA((2,)),
-        ],
+        scratch_shapes=[pltpu.VMEM((count * height, features), BF16)],
         compiler_params=small_grant(),
         cost_estimate=pl.CostEstimate(
             flops=2 * count * height * features * columns, bytes_accessed=2 * features * columns, transcendentals=0
         ),
-    )(*blocks, in_hbm(own), other)
+    )(*blocks, weight)
 
 
 def shared_down_kernel(blocks_ref, own_hbm, other_hbm, out_ref, rows_ref, weight_ref, sems):
@@ -443,7 +455,9 @@
         return lax.all_to_all(value, "expert", 0, 0, axis_index_groups=groups, tiled=True)
 
     own_up, own_down = shared_gate_up[0], jnp.swapaxes(shared_down[0], 0, 1)
-    other_up, other_down = swap(own_up, 1), swap(own_down, 1)
+    other_up = swap(own_up, 1)
+    other_down = swap(own_down, 1)
+    near_up = pair_up(own_up, other_up)
     payload = make_payload(tokens, live, expert_ids, gate_weights, norm_gain, EXPERTS)
     along = [payload] + swap_line([payload] * (line_count - 1))
     across = []
@@ -453,7 +467,7 @@
     masks = [2 * k for k in range(line_count)] + [2 * k + 1 for k in range(line_count)]
     beside = [swap(block, 1) for block in same]
 
-    partial_value = shared_up(same, masks, own_up, other_up)
+    partial_value = shared_up(same, masks, near_up)
     width, features = tokens.shape[2], 2 * own_down.shape[0]
     unit = features if features % LANES == 0 else LANES
     first_width = (width // unit * FIRST_EIGHTHS + 4) // 8 * unit

time: 85.4 us -> 83.5 us (0.978)
  waiting for transfers between devices: 25.2 us -> 23.2 us
    ppermute x27, waiting for transfers between devices: 17.9 us -> 15.8 us  [swap(): lax.ppermute(value, 'expert', [(i, i ^ mask) for i in range(device_count)])]
    pallas_call x0 -> x1, Pallas kernels: none -> 1.52 us  [pair_up(): pl.pallas_call(pair_kernel, out_shape=pltpu.VMEM((2 * rows, columns), BF1...]
    pallas_call x1, Pallas kernels: 2.97 us -> 1.47 us  [shared_up(): pl.pallas_call(functools.partial(shared_up_kernel, masks), out_shape=jax....]
  transfers between devices with their start and end apart: 29 -> 29, of which waited for: 8 -> 7; matrix products, arithmetic and copies ran while one was open for 0% -> 0% of each run, Pallas kernels for 28% -> 29%
where the time goes in v1:
time: 83.5 us; the launch traced here: 83.1 us
  starting transfers between devices  34.3 us (41%)
  Pallas kernels  24.7 us (30%)
  waiting for transfers between devices  23.2 us (28%)
    ppermute x27, starting transfers between devices, swap(): lax.ppermute(value, 'expert', [(i, i ^ mask) for i in range(device_count)])  22.5 us
    ppermute x27, waiting for transfers between devices, swap(): lax.ppermute(value, 'expert', [(i, i ^ mask) for i in range(device_count)])  15.8 us
    all_to_all x2, starting transfers between devices, exchange(): lax.all_to_all(value, 'expert', 0, 0, axis_index_groups=groups, tiled=True)  11.8 us
    pallas_call x1, Pallas kernels, routed_up(): pl.pallas_call(functools.partial(routed_up_kernel, len(blocks), expert_co...  10.3 us
    all_to_all x2, waiting for transfers between devices, exchange(): lax.all_to_all(value, 'expert', 0, 0, axis_index_groups=groups, tiled=True)  7.33 us
    pallas_call x1, Pallas kernels, routed_down(): pl.pallas_call(functools.partial(routed_down_kernel, step, len(widths)),...  6.6 us
    pallas_call x1, Pallas kernels, shared_down_rows(): pl.pallas_call(shared_down_kernel, out_shape=jax.ShapeDtypeStruct((count,...  1.87 us
  transfers between devices with their start and end apart: 29, of which 7 were waited for; matrix products, arithmetic and copies ran while one was open for 0% of the time, Pallas kernels for 29%

profile of v1, /device:TPU:0, one launch (start us, length us, event | category | flops | bytes accessed | tf_op | source)
XLA Modules:
  0.0 83.1 jit_solution(1150492653076607811)
XLA Ops:
  0.0 0.5 collective-permute-start.15
  0.5 1.2 %shard_map.91.refs_0_ = bf16[8,7296]{1,0:T(8,128)(2,1)S(1)} custom-call(s32[1,2]{1,0:T(1,128)} %bitcast.7, bf16[2,4,7168]{2,1,0:T(4,128)(2,1)} %tokens_ref.1, s32[1,2,4,8]{3,2,1,0:T(4,128)} %refs_2_.1, f32[1,2,4,8]{3,2,1,0:T(4,128)} %refs_3_.1, f32[1,7168]{1,0:T(1,128)} %refs_4_.1), custom_call_target="tpu_custom_call" | custom-call | flops 458752 | bytes 344064 | tf_op jit(solution)/shard_map/pallas_call | solution.py:92
  1.7 2.6 %collective-permute-start = (bf16[8,7296]{1,0:T(8,128)(2,1)S(1)}, bf16[8,7296]{1,0:T(8,128)(2,1)S(1)}, u32[]{:S(2)}, u32[]{:S(2)}) collective-permute-start(bf16[8,7296]{1,0:T(8,128)(2,1)S(1)} %shard_map.91.refs_0_), channel_id=1, source_target_pairs={{0,4},{1,5},{2,6},{3,7},{4,0},{5,1},{6,2},{7,3},{8,12},{9,13},{10,... | collective-permute-start | bytes 350216 | tf_op jit(solution)/shard_map/ppermute | solution.py:444
  4.3 2.6 %collective-permute-start.1 = (bf16[8,7296]{1,0:T(8,128)(2,1)S(1)}, bf16[8,7296]{1,0:T(8,128)(2,1)S(1)}, u32[]{:S(2)}, u32[]{:S(2)}) collective-permute-start(bf16[8,7296]{1,0:T(8,128)(2,1)S(1)} %shard_map.91.refs_0_), channel_id=1, source_target_pairs={{0,8},{1,9},{2,10},{3,11},{4,12},{5,13},{6,14},{7,15},{8,0},{9,1},... | collective-permute-start | bytes 350216 | tf_op jit(solution)/shard_map/ppermute | solution.py:444
  6.9 0.0 collective-permute-start.2
  6.9 1.7 %collective-permute-start.3 = (bf16[8,7296]{1,0:T(8,128)(2,1)S(1)}, bf16[8,7296]{1,0:T(8,128)(2,1)S(1)}, u32[]{:S(2)}, u32[]{:S(2)}) collective-permute-start(bf16[8,7296]{1,0:T(8,128)(2,1)S(1)} %shard_map.91.refs_0_), channel_id=1, source_target_pairs={{0,2},{1,3},{2,0},{3,1},{4,6},{5,7},{6,4},{7,5},{8,10},{9,11},{10,... | collective-permute-start | bytes 350216 | tf_op jit(solution)/shard_map/ppermute | solution.py:444
  8.6 1.3 %collective-permute-done.refs_1_ = bf16[8,7296]{1,0:T(8,128)(2,1)S(1)} collective-permute-done((bf16[8,7296]{1,0:T(8,128)(2,1)S(1)}, bf16[8,7296]{1,0:T(8,128)(2,1)S(1)}, u32[]{:S(2)}, u32[]{:S(2)}) %collective-permute-start) | collective-permute-done | bytes 116768 | tf_op jit(solution)/shard_map/ppermute | solution.py:444
  10.0 0.0 collective-permute-start.7
  10.0 6.3 %collective-permute-done.1.refs_2_ = bf16[8,7296]{1,0:T(8,128)(2,1)S(1)} collective-permute-done((bf16[8,7296]{1,0:T(8,128)(2,1)S(1)}, bf16[8,7296]{1,0:T(8,128)(2,1)S(1)}, u32[]{:S(2)}, u32[]{:S(2)}) %collective-permute-start.1) | collective-permute-done | bytes 116768 | tf_op jit(solution)/shard_map/ppermute | solution.py:444
  16.3 1.5 %collective-permute-start.4 = (bf16[8,7296]{1,0:T(8,128)(2,1)S(1)}, bf16[8,7296]{1,0:T(8,128)(2,1)S(1)}, u32[]{:S(2)}, u32[]{:S(2)}) collective-permute-start(bf16[8,7296]{1,0:T(8,128)(2,1)S(1)} %collective-permute-done.refs_1_), channel_id=1, source_target_pairs={{0,2},{1,3},{2,0},{3,1},{4,6},{5,7},{6,4},{7,5},{8,10},{9,11},{10,... | collective-permute-start | bytes 350216 | tf_op jit(solution)/shard_map/ppermute | solution.py:444
  17.8 0.0 collective-permute-done.2.refs_3_
  17.8 0.5 collective-permute-start.5
  18.3 0.0 collective-permute-done.3.refs_4_
  18.3 1.5 %collective-permute-start.6 = (bf16[8,7296]{1,0:T(8,128)(2,1)S(1)}, bf16[8,7296]{1,0:T(8,128)(2,1)S(1)}, u32[]{:S(2)}, u32[]{:S(2)}) collective-permute-start(bf16[8,7296]{1,0:T(8,128)(2,1)S(1)} %collective-permute-done.2.refs_3_), channel_id=1, source_target_pairs={{0,2},{1,3},{2,0},{3,1},{4,6},{5,7},{6,4},{7,5},{8,10},{9,11},{10,... | collective-permute-start | bytes 350216 | tf_op jit(solution)/shard_map/ppermute | solution.py:444
  19.9 0.0 collective-permute-done.7.refs_8_
  19.9 0.0 collective-permute-start.10
  19.9 0.0 collective-permute-done.15.other_hbm
  19.9 0.5 collective-permute-start.8
  20.4 1.5 %shard_map.92.refs_8_ = bf16[896,2048]{1,0:T(8,128)(2,1)S(1)} custom-call(bf16[448,2048]{1,0:T(8,128)(2,1)} %bitcast.12, bf16[448,2048]{1,0:T(8,128)(2,1)S(1)} %collective-permute-done.15.other_hbm), custom_call_target="tpu_custom_call" | custom-call | bytes 3670016 | tf_op jit(solution)/shard_map/pallas_call | solution.py:175
  21.9 0.0 collective-permute-done.4.refs_5_
  21.9 0.1 collective-permute-start.9
  22.1 0.6 collective-permute-done.5.refs_6_
  22.6 0.0 collective-permute-start.11
  22.6 1.2 %collective-permute-done.6.refs_7_ = bf16[8,7296]{1,0:T(8,128)(2,1)S(1)} collective-permute-done((bf16[8,7296]{1,0:T(8,128)(2,1)S(1)}, bf16[8,7296]{1,0:T(8,128)(2,1)S(1)}, u32[]{:S(2)}, u32[]{:S(2)}) %collective-permute-start.6) | collective-permute-done | bytes 116768 | tf_op jit(solution)/shard_map/ppermute | solution.py:444
  23.9 0.0 collective-permute-start.12
  23.9 0.5 collective-permute-start.13
  24.4 0.1 collective-permute-start.14
  24.5 1.5 %shard_map.93 = bf16[8,8,2048]{2,1,0:T(8,128)(2,1)} custom-call(bf16[8,7296]{1,0:T(8,128)(2,1)S(1)} %shard_map.91.refs_0_, bf16[8,7296]{1,0:T(8,128)(2,1)S(1)} %collective-permute-done.refs_1_, bf16[8,7296]{1,0:T(8,128)(2,1)S(1)} %collective-permute-done.1.refs_2_, bf16[8,7296]{1,0:T(8,128)(2,1)S(1)} %collective-permute-done.2.refs_3_, ...), custom_call_target="tpu_custom_call" | custom-call | flops 234881024 | bytes 3670016 | tf_op jit(solution)/shard_map/pallas_call | solution.py:206
  26.0 5.8 %all-to-all-start = ((bf16[8,8,2048]{2,1,0:T(8,128)(2,1)}), bf16[8,8,2048]{2,1,0:T(8,128)(2,1)S(1)}, u32[]{:S(2)}, u32[]{:S(2)}) async-start(bf16[8,8,2048]{2,1,0:T(8,128)(2,1)} %shard_map.93), calls=%async_computation | async-start | bytes 524288 | tf_op jit(solution)/shard_map/all_to_all | solution.py:455
  31.8 0.0 collective-permute-done.9.refs_10_
  31.8 0.2 collective-permute-start.17
  32.0 0.0 collective-permute-done.11.refs_12_
  32.0 0.0 collective-permute-done.12.refs_13_
  32.0 0.0 collective-permute-done.13.refs_14_
  32.0 0.0 collective-permute-done.14.refs_15_
  32.1 10.3 %shard_map.94 = (bf16[128,1024]{1,0:T(8,128)(2,1)S(1)}, f32[128,128]{1,0:T(8,128)S(1)}) custom-call(bf16[8,7296]{1,0:T(8,128)(2,1)S(1)} %shard_map.91.refs_0_, bf16[8,7296]{1,0:T(8,128)(2,1)S(1)} %collective-permute-done.refs_1_, bf16[8,7296]{1,0:T(8,128)(2,1)S(1)} %collective-permute-done.1.refs_2_, bf16[8,7296]{1,0:T(8,128)(2,1)S(1)} %collective-permute-done.2.refs_3_, ...), custom_call_target="tpu_custom_call" | custom-call | flops 3758096384 | bytes 29360128 | tf_op jit(solution)/shard_map/pallas_call | solution.py:323
  42.4 0.7 shard_map.95
  43.0 6.6 %shard_map.96 = (bf16[64,4480]{1,0:T(8,128)(2,1)S(1)}, bf16[64,4480]{1,0:T(8,128)(2,1)}, bf16[64,2688]{1,0:T(8,128)(2,1)S(1)}, bf16[64,2688]{1,0:T(8,128)(2,1)S(1)}) custom-call(bf16[128,1024]{1,0:T(8,128)(2,1)S(1)} %get-tuple-element.28.hidden_ref, f32[128,128]{1,0:T(8,128)S(1)} %get-tuple-element.29.gate_ref, bf16[1024,7168]{1,0:T(8,128)(2,1)} %bitcast.10), custom_call_target="tpu_custom_call" | custom-call | flops 1879048192 | bytes 14680064 | tf_op jit(solution)/shard_map/pallas_call | solution.py:383
  49.7 0.8 copy-done.2
  50.4 0.3 collective-permute-start.16
  50.8 5.9 %all-to-all-start.1 = ((bf16[8,8,1024]{2,1,0:T(8,128)(2,1)}), bf16[8,8,1024]{2,1,0:T(8,128)(2,1)S(1)}, u32[]{:S(2)}, u32[]{:S(2)}) async-start(bf16[8,8,1024]{2,1,0:T(8,128)(2,1)} %shard_map.95), calls=%async_computation.1 | async-start | bytes 262144 | tf_op jit(solution)/shard_map/all_to_all | solution.py:455
  56.7 7.3 %all-to-all-done.1.blocks_ref = bf16[8,8,1024]{2,1,0:T(8,128)(2,1)S(1)} async-done(((bf16[8,8,1024]{2,1,0:T(8,128)(2,1)}), bf16[8,8,1024]{2,1,0:T(8,128)(2,1)S(1)}, u32[]{:S(2)}, u32[]{:S(2)}) %all-to-all-start.1) | async-done | bytes 131104 | tf_op jit(solution)/shard_map/all_to_all | solution.py:455
  64.0 1.9 %shard_map.97.refs_2_ = bf16[8,8,896]{2,1,0:T(8,128)(2,1)S(1)} custom-call(bf16[8,8,1024]{2,1,0:T(8,128)(2,1)S(1)} %all-to-all-done.1.blocks_ref, bf16[448,1024]{1,0:T(8,128)(2,1)} %bitcast.14, bf16[448,1024]{1,0:T(8,128)(2,1)S(1)} %collective-permute-done.17.other_hbm), custom_call_target="tpu_custom_call" | custom-call | flops 117440512 | bytes 1835008 | tf_op jit(solution)/shard_map/pallas_call | solution.py:237
  65.9 0.0 collective-permute-done.16.refs_1_
  65.9 0.2 shard_map.98
  66.1 0.4 collective-permute-start.18
  66.5 0.0 collective-permute-done.22.refs_1_
  66.5 0.1 shard_map.100
  66.6 1.0 %collective-permute-start.23 = (bf16[16,2688]{1,0:T(8,128)(2,1)S(1)}, bf16[16,2688]{1,0:T(8,128)(2,1)S(1)}, u32[]{:S(2)}, u32[]{:S(2)}) collective-permute-start(bf16[16,2688]{1,0:T(8,128)(2,1)S(1)} %get-tuple-element.44), channel_id=1, source_target_pairs={{0,4},{1,5},{2,6},{3,7},{4,0},{5,1},{6,2},{7,3},{8,12},{9,13},{10,... | collective-permute-start | bytes 258056 | tf_op jit(solution)/shard_map/ppermute | solution.py:444
  67.6 1.2 %collective-permute-start.24 = (bf16[16,2688]{1,0:T(8,128)(2,1)S(1)}, bf16[16,2688]{1,0:T(8,128)(2,1)S(1)}, u32[]{:S(2)}, u32[]{:S(2)}) collective-permute-start(bf16[16,2688]{1,0:T(8,128)(2,1)S(1)} %get-tuple-element.45), channel_id=1, source_target_pairs={{0,8},{1,9},{2,10},{3,11},{4,12},{5,13},{6,14},{7,15},{8,0},{9,1},... | collective-permute-start | bytes 258056 | tf_op jit(solution)/shard_map/ppermute | solution.py:444
  68.9 2.2 %collective-permute-start.25 = (bf16[16,2688]{1,0:T(8,128)(2,1)S(1)}, bf16[16,2688]{1,0:T(8,128)(2,1)S(1)}, u32[]{:S(2)}, u32[]{:S(2)}) collective-permute-start(bf16[16,2688]{1,0:T(8,128)(2,1)S(1)} %get-tuple-element.46), channel_id=1, source_target_pairs={{0,12},{1,13},{2,14},{3,15},{4,8},{5,9},{6,10},{7,11},{8,4},{9,5},... | collective-permute-start | bytes 258056 | tf_op jit(solution)/shard_map/ppermute | solution.py:444
  71.1 2.6 %collective-permute-done.18.refs_1_ = bf16[32,4480]{1,0:T(8,128)(2,1)S(1)} collective-permute-done((bf16[32,4480]{1,0:T(8,128)(2,1)S(1)}, bf16[32,4480]{1,0:T(8,128)(2,1)S(1)}, u32[]{:S(2)}, u32[]{:S(2)}) %collective-permute-start.18) | collective-permute-done | bytes 286752 | tf_op jit(solution)/shard_map/ppermute | solution.py:444
  73.6 0.1 shard_map.99
  73.7 0.2 collective-permute-start.19
  73.9 1.7 %collective-permute-start.20 = (bf16[8,4480]{1,0:T(8,128)(2,1)S(1)}, bf16[8,4480]{1,0:T(8,128)(2,1)S(1)}, u32[]{:S(2)}, u32[]{:S(2)}) collective-permute-start(bf16[8,4480]{1,0:T(8,128)(2,1)S(1)} %get-tuple-element.39), channel_id=1, source_target_pairs={{0,8},{1,9},{2,10},{3,11},{4,12},{5,13},{6,14},{7,15},{8,0},{9,1},... | collective-permute-start | bytes 215048 | tf_op jit(solution)/shard_map/ppermute | solution.py:444
  75.6 2.6 %collective-permute-start.21 = (bf16[8,4480]{1,0:T(8,128)(2,1)S(1)}, bf16[8,4480]{1,0:T(8,128)(2,1)S(1)}, u32[]{:S(2)}, u32[]{:S(2)}) collective-permute-start(bf16[8,4480]{1,0:T(8,128)(2,1)S(1)} %get-tuple-element.40), channel_id=1, source_target_pairs={{0,12},{1,13},{2,14},{3,15},{4,8},{5,9},{6,10},{7,11},{8,4},{9,5},... | collective-permute-start | bytes 215048 | tf_op jit(solution)/shard_map/ppermute | solution.py:444
  78.2 0.0 collective-permute-done.24.refs_2_
  78.2 0.0 collective-permute-done.25.refs_3_
  78.2 0.4 collective-permute-start.26
  78.6 3.7 %collective-permute-done.26.refs_5_ = bf16[8,2688]{1,0:T(8,128)(2,1)S(1)} collective-permute-done((bf16[8,2688]{1,0:T(8,128)(2,1)S(1)}, bf16[8,2688]{1,0:T(8,128)(2,1)S(1)}, u32[]{:S(2)}, u32[]{:S(2)}) %collective-permute-start.26) | collective-permute-done | bytes 43040 | tf_op jit(solution)/shard_map/ppermute | solution.py:444
  82.3 0.0 collective-permute-done.19.refs_1_
  82.3 0.0 collective-permute-done.20.refs_2_
  82.3 0.0 collective-permute-done.21.refs_3_
  82.4 0.8 shard_map.102
  (12 shorter events, 0.1 us)
Async XLA Ops:
  0.0 19.9 %collective-permute-start.15 = (bf16[448,2048]{1,0:T(8,128)(2,1)}, bf16[448,2048]{1,0:T(8,128)(2,1)S(1)}, u32[]{:S(2)}, u32[]{:S(2)}) collective-permute-start(bf16[448,2048]{1,0:T(8,128)(2,1)} %bitcast.11), channel_id=1, source_target_pairs={{0,1},{1,0},{2,3},{3,2},{4,5},{5,4},{6,7},{7,6},{8,9},{9,8},{10,11... | collective-permute-start | bytes 5505032 | tf_op jit(solution)/shard_map/ppermute | solution.py:444
  1.7 8.3 %collective-permute-start = (bf16[8,7296]{1,0:T(8,128)(2,1)S(1)}, bf16[8,7296]{1,0:T(8,128)(2,1)S(1)}, u32[]{:S(2)}, u32[]{:S(2)}) collective-permute-start(bf16[8,7296]{1,0:T(8,128)(2,1)S(1)} %shard_map.91.refs_0_), channel_id=1, source_target_pairs={{0,4},{1,5},{2,6},{3,7},{4,0},{5,1},{6,2},{7,3},{8,12},{9,13},{10,... | collective-permute-start | bytes 350216 | tf_op jit(solution)/shard_map/ppermute | solution.py:444
  4.3 12.0 %collective-permute-start.1 = (bf16[8,7296]{1,0:T(8,128)(2,1)S(1)}, bf16[8,7296]{1,0:T(8,128)(2,1)S(1)}, u32[]{:S(2)}, u32[]{:S(2)}) collective-permute-start(bf16[8,7296]{1,0:T(8,128)(2,1)S(1)} %shard_map.91.refs_0_), channel_id=1, source_target_pairs={{0,8},{1,9},{2,10},{3,11},{4,12},{5,13},{6,14},{7,15},{8,0},{9,1},... | collective-permute-start | bytes 350216 | tf_op jit(solution)/shard_map/ppermute | solution.py:444
  6.9 10.9 %collective-permute-start.2 = (bf16[8,7296]{1,0:T(8,128)(2,1)S(1)}, bf16[8,7296]{1,0:T(8,128)(2,1)S(1)}, u32[]{:S(2)}, u32[]{:S(2)}) collective-permute-start(bf16[8,7296]{1,0:T(8,128)(2,1)S(1)} %shard_map.91.refs_0_), channel_id=1, source_target_pairs={{0,12},{1,13},{2,14},{3,15},{4,8},{5,9},{6,10},{7,11},{8,4},{9,5},... | collective-permute-start | bytes 350216 | tf_op jit(solution)/shard_map/ppermute | solution.py:444
  6.9 11.5 %collective-permute-start.3 = (bf16[8,7296]{1,0:T(8,128)(2,1)S(1)}, bf16[8,7296]{1,0:T(8,128)(2,1)S(1)}, u32[]{:S(2)}, u32[]{:S(2)}) collective-permute-start(bf16[8,7296]{1,0:T(8,128)(2,1)S(1)} %shard_map.91.refs_0_), channel_id=1, source_target_pairs={{0,2},{1,3},{2,0},{3,1},{4,6},{5,7},{6,4},{7,5},{8,10},{9,11},{10,... | collective-permute-start | bytes 350216 | tf_op jit(solution)/shard_map/ppermute | solution.py:444
  10.0 9.9 %collective-permute-start.7 = (bf16[8,7296]{1,0:T(8,128)(2,1)S(1)}, bf16[8,7296]{1,0:T(8,128)(2,1)S(1)}, u32[]{:S(2)}, u32[]{:S(2)}) collective-permute-start(bf16[8,7296]{1,0:T(8,128)(2,1)S(1)} %shard_map.91.refs_0_), channel_id=1, source_target_pairs={{0,1},{1,0},{2,3},{3,2},{4,5},{5,4},{6,7},{7,6},{8,9},{9,8},{10,11... | collective-permute-start | bytes 350216 | tf_op jit(solution)/shard_map/ppermute | solution.py:444
  16.3 5.6 %collective-permute-start.4 = (bf16[8,7296]{1,0:T(8,128)(2,1)S(1)}, bf16[8,7296]{1,0:T(8,128)(2,1)S(1)}, u32[]{:S(2)}, u32[]{:S(2)}) collective-permute-start(bf16[8,7296]{1,0:T(8,128)(2,1)S(1)} %collective-permute-done.refs_1_), channel_id=1, source_target_pairs={{0,2},{1,3},{2,0},{3,1},{4,6},{5,7},{6,4},{7,5},{8,10},{9,11},{10,... | collective-permute-start | bytes 350216 | tf_op jit(solution)/shard_map/ppermute | solution.py:444
  17.8 4.8 %collective-permute-start.5 = (bf16[8,7296]{1,0:T(8,128)(2,1)S(1)}, bf16[8,7296]{1,0:T(8,128)(2,1)S(1)}, u32[]{:S(2)}, u32[]{:S(2)}) collective-permute-start(bf16[8,7296]{1,0:T(8,128)(2,1)S(1)} %collective-permute-done.1.refs_2_), channel_id=1, source_target_pairs={{0,2},{1,3},{2,0},{3,1},{4,6},{5,7},{6,4},{7,5},{8,10},{9,11},{10,... | collective-permute-start | bytes 350216 | tf_op jit(solution)/shard_map/ppermute | solution.py:444
  18.3 5.6 %collective-permute-start.6 = (bf16[8,7296]{1,0:T(8,128)(2,1)S(1)}, bf16[8,7296]{1,0:T(8,128)(2,1)S(1)}, u32[]{:S(2)}, u32[]{:S(2)}) collective-permute-start(bf16[8,7296]{1,0:T(8,128)(2,1)S(1)} %collective-permute-done.2.refs_3_), channel_id=1, source_target_pairs={{0,2},{1,3},{2,0},{3,1},{4,6},{5,7},{6,4},{7,5},{8,10},{9,11},{10,... | collective-permute-start | bytes 350216 | tf_op jit(solution)/shard_map/ppermute | solution.py:444
  19.9 4.0 %collective-permute-start.10 = (bf16[8,7296]{1,0:T(8,128)(2,1)S(1)}, bf16[8,7296]{1,0:T(8,128)(2,1)S(1)}, u32[]{:S(2)}, u32[]{:S(2)}) collective-permute-start(bf16[8,7296]{1,0:T(8,128)(2,1)S(1)} %collective-permute-done.2.refs_3_), channel_id=1, source_target_pairs={{0,1},{1,0},{2,3},{3,2},{4,5},{5,4},{6,7},{7,6},{8,9},{9,8},{10,11... | collective-permute-start | bytes 350216 | tf_op jit(solution)/shard_map/ppermute | solution.py:444
  19.9 4.5 %collective-permute-start.8 = (bf16[8,7296]{1,0:T(8,128)(2,1)S(1)}, bf16[8,7296]{1,0:T(8,128)(2,1)S(1)}, u32[]{:S(2)}, u32[]{:S(2)}) collective-permute-start(bf16[8,7296]{1,0:T(8,128)(2,1)S(1)} %collective-permute-done.refs_1_), channel_id=1, source_target_pairs={{0,1},{1,0},{2,3},{3,2},{4,5},{5,4},{6,7},{7,6},{8,9},{9,8},{10,11... | collective-permute-start | bytes 350216 | tf_op jit(solution)/shard_map/ppermute | solution.py:444
  21.9 9.9 %collective-permute-start.9 = (bf16[8,7296]{1,0:T(8,128)(2,1)S(1)}, bf16[8,7296]{1,0:T(8,128)(2,1)S(1)}, u32[]{:S(2)}, u32[]{:S(2)}) collective-permute-start(bf16[8,7296]{1,0:T(8,128)(2,1)S(1)} %collective-permute-done.1.refs_2_), channel_id=1, source_target_pairs={{0,1},{1,0},{2,3},{3,2},{4,5},{5,4},{6,7},{7,6},{8,9},{9,8},{10,11... | collective-permute-start | bytes 350216 | tf_op jit(solution)/shard_map/ppermute | solution.py:444
  22.6 9.4 %collective-permute-start.11 = (bf16[8,7296]{1,0:T(8,128)(2,1)S(1)}, bf16[8,7296]{1,0:T(8,128)(2,1)S(1)}, u32[]{:S(2)}, u32[]{:S(2)}) collective-permute-start(bf16[8,7296]{1,0:T(8,128)(2,1)S(1)} %collective-permute-done.3.refs_4_), channel_id=1, source_target_pairs={{0,1},{1,0},{2,3},{3,2},{4,5},{5,4},{6,7},{7,6},{8,9},{9,8},{10,11... | collective-permute-start | bytes 350216 | tf_op jit(solution)/shard_map/ppermute | solution.py:444
  23.9 8.1 %collective-permute-start.12 = (bf16[8,7296]{1,0:T(8,128)(2,1)S(1)}, bf16[8,7296]{1,0:T(8,128)(2,1)S(1)}, u32[]{:S(2)}, u32[]{:S(2)}) collective-permute-start(bf16[8,7296]{1,0:T(8,128)(2,1)S(1)} %collective-permute-done.4.refs_5_), channel_id=1, source_target_pairs={{0,1},{1,0},{2,3},{3,2},{4,5},{5,4},{6,7},{7,6},{8,9},{9,8},{10,11... | collective-permute-start | bytes 350216 | tf_op jit(solution)/shard_map/ppermute | solution.py:444
  23.9 8.1 %collective-permute-start.13 = (bf16[8,7296]{1,0:T(8,128)(2,1)S(1)}, bf16[8,7296]{1,0:T(8,128)(2,1)S(1)}, u32[]{:S(2)}, u32[]{:S(2)}) collective-permute-start(bf16[8,7296]{1,0:T(8,128)(2,1)S(1)} %collective-permute-done.5.refs_6_), channel_id=1, source_target_pairs={{0,1},{1,0},{2,3},{3,2},{4,5},{5,4},{6,7},{7,6},{8,9},{9,8},{10,11... | collective-permute-start | bytes 350216 | tf_op jit(solution)/shard_map/ppermute | solution.py:444
  24.4 7.6 %collective-permute-start.14 = (bf16[8,7296]{1,0:T(8,128)(2,1)S(1)}, bf16[8,7296]{1,0:T(8,128)(2,1)S(1)}, u32[]{:S(2)}, u32[]{:S(2)}) collective-permute-start(bf16[8,7296]{1,0:T(8,128)(2,1)S(1)} %collective-permute-done.6.refs_7_), channel_id=1, source_target_pairs={{0,1},{1,0},{2,3},{3,2},{4,5},{5,4},{6,7},{7,6},{8,9},{9,8},{10,11... | collective-permute-start | bytes 350216 | tf_op jit(solution)/shard_map/ppermute | solution.py:444
  26.0 16.4 %all-to-all-start = ((bf16[8,8,2048]{2,1,0:T(8,128)(2,1)}), bf16[8,8,2048]{2,1,0:T(8,128)(2,1)S(1)}, u32[]{:S(2)}, u32[]{:S(2)}) async-start(bf16[8,8,2048]{2,1,0:T(8,128)(2,1)} %shard_map.93), calls=%async_computation | async-start | bytes 524288 | tf_op jit(solution)/shard_map/all_to_all | solution.py:455
  31.8 24.9 %collective-permute-start.17 = (bf16[448,1024]{1,0:T(8,128)(2,1)}, bf16[448,1024]{1,0:T(8,128)(2,1)S(1)}, u32[]{:S(2)}, u32[]{:S(2)}) collective-permute-start(bf16[448,1024]{1,0:T(8,128)(2,1)} %bitcast.13), channel_id=1, source_target_pairs={{0,1},{1,0},{2,3},{3,2},{4,5},{5,4},{6,7},{7,6},{8,9},{9,8},{10,11... | collective-permute-start | bytes 2752520 | tf_op jit(solution)/shard_map/ppermute | solution.py:444
  49.7 0.8 copy-start.2
  50.4 31.9 %copy-start = (bf16[2,4,7168]{2,1,0:T(4,128)(2,1)S(1)}, bf16[2,4,7168]{2,1,0:T(4,128)(2,1)}, u32[]{:S(2)}) copy-start(bf16[2,4,7168]{2,1,0:T(4,128)(2,1)} %tokens_ref.1) | copy-start | bytes 344068
  50.4 31.9 %copy-start.1 = (s32[2,1]{0,1:T(1,128)S(1)}, s32[2,1]{0,1:T(1,128)}, u32[]{:S(2)}) copy-start(s32[2,1]{0,1:T(1,128)} %param.10) | copy-start | bytes 28
  50.4 15.5 %collective-permute-start.16 = (bf16[64,4480]{1,0:T(8,128)(2,1)}, bf16[64,4480]{1,0:T(8,128)(2,1)S(1)}, u32[]{:S(2)}, u32[]{:S(2)}) collective-permute-start(bf16[64,4480]{1,0:T(8,128)(2,1)} %get-tuple-element.33), channel_id=1, source_target_pairs={{0,1},{1,0},{2,3},{3,2},{4,5},{5,4},{6,7},{7,6},{8,9},{9,8},{10,11... | collective-permute-start | bytes 1720328 | tf_op jit(solution)/shard_map/ppermute | solution.py:444
  50.8 13.3 %all-to-all-start.1 = ((bf16[8,8,1024]{2,1,0:T(8,128)(2,1)}), bf16[8,8,1024]{2,1,0:T(8,128)(2,1)S(1)}, u32[]{:S(2)}, u32[]{:S(2)}) async-start(bf16[8,8,1024]{2,1,0:T(8,128)(2,1)} %shard_map.95), calls=%async_computation.1 | async-start | bytes 262144 | tf_op jit(solution)/shard_map/all_to_all | solution.py:455
  56.7 9.8 %collective-permute-start.22 = (bf16[64,2688]{1,0:T(8,128)(2,1)}, bf16[64,2688]{1,0:T(8,128)(2,1)S(1)}, u32[]{:S(2)}, u32[]{:S(2)}) collective-permute-start(bf16[64,2688]{1,0:T(8,128)(2,1)} %copy-done.2), channel_id=1, source_target_pairs={{0,1},{1,0},{2,3},{3,2},{4,5},{5,4},{6,7},{7,6},{8,9},{9,8},{10,11... | collective-permute-start | bytes 1032200 | tf_op jit(solution)/shard_map/ppermute | solution.py:444
  66.1 7.5 %collective-permute-start.18 = (bf16[32,4480]{1,0:T(8,128)(2,1)S(1)}, bf16[32,4480]{1,0:T(8,128)(2,1)S(1)}, u32[]{:S(2)}, u32[]{:S(2)}) collective-permute-start(bf16[32,4480]{1,0:T(8,128)(2,1)S(1)} %get-tuple-element.36), channel_id=1, source_target_pairs={{0,2},{1,3},{2,0},{3,1},{4,6},{5,7},{6,4},{7,5},{8,10},{9,11},{10,... | collective-permute-start | bytes 860168 | tf_op jit(solution)/shard_map/ppermute | solution.py:444
  66.6 9.0 %collective-permute-start.23 = (bf16[16,2688]{1,0:T(8,128)(2,1)S(1)}, bf16[16,2688]{1,0:T(8,128)(2,1)S(1)}, u32[]{:S(2)}, u32[]{:S(2)}) collective-permute-start(bf16[16,2688]{1,0:T(8,128)(2,1)S(1)} %get-tuple-element.44), channel_id=1, source_target_pairs={{0,4},{1,5},{2,6},{3,7},{4,0},{5,1},{6,2},{7,3},{8,12},{9,13},{10,... | collective-permute-start | bytes 258056 | tf_op jit(solution)/shard_map/ppermute | solution.py:444
  67.6 10.5 %collective-permute-start.24 = (bf16[16,2688]{1,0:T(8,128)(2,1)S(1)}, bf16[16,2688]{1,0:T(8,128)(2,1)S(1)}, u32[]{:S(2)}, u32[]{:S(2)}) collective-permute-start(bf16[16,2688]{1,0:T(8,128)(2,1)S(1)} %get-tuple-element.45), channel_id=1, source_target_pairs={{0,8},{1,9},{2,10},{3,11},{4,12},{5,13},{6,14},{7,15},{8,0},{9,1},... | collective-permute-start | bytes 258056 | tf_op jit(solution)/shard_map/ppermute | solution.py:444
  68.9 9.3 %collective-permute-start.25 = (bf16[16,2688]{1,0:T(8,128)(2,1)S(1)}, bf16[16,2688]{1,0:T(8,128)(2,1)S(1)}, u32[]{:S(2)}, u32[]{:S(2)}) collective-permute-start(bf16[16,2688]{1,0:T(8,128)(2,1)S(1)} %get-tuple-element.46), channel_id=1, source_target_pairs={{0,12},{1,13},{2,14},{3,15},{4,8},{5,9},{6,10},{7,11},{8,4},{9,5},... | collective-permute-start | bytes 258056 | tf_op jit(solution)/shard_map/ppermute | solution.py:444
  73.7 8.6 %collective-permute-start.19 = (bf16[8,4480]{1,0:T(8,128)(2,1)S(1)}, bf16[8,4480]{1,0:T(8,128)(2,1)S(1)}, u32[]{:S(2)}, u32[]{:S(2)}) collective-permute-start(bf16[8,4480]{1,0:T(8,128)(2,1)S(1)} %get-tuple-element.38), channel_id=1, source_target_pairs={{0,4},{1,5},{2,6},{3,7},{4,0},{5,1},{6,2},{7,3},{8,12},{9,13},{10,... | collective-permute-start | bytes 215048 | tf_op jit(solution)/shard_map/ppermute | solution.py:444
  73.9 8.4 %collective-permute-start.20 = (bf16[8,4480]{1,0:T(8,128)(2,1)S(1)}, bf16[8,4480]{1,0:T(8,128)(2,1)S(1)}, u32[]{:S(2)}, u32[]{:S(2)}) collective-permute-start(bf16[8,4480]{1,0:T(8,128)(2,1)S(1)} %get-tuple-element.39), channel_id=1, source_target_pairs={{0,8},{1,9},{2,10},{3,11},{4,12},{5,13},{6,14},{7,15},{8,0},{9,1},... | collective-permute-start | bytes 215048 | tf_op jit(solution)/shard_map/ppermute | solution.py:444
  75.6 6.7 %collective-permute-start.21 = (bf16[8,4480]{1,0:T(8,128)(2,1)S(1)}, bf16[8,4480]{1,0:T(8,128)(2,1)S(1)}, u32[]{:S(2)}, u32[]{:S(2)}) collective-permute-start(bf16[8,4480]{1,0:T(8,128)(2,1)S(1)} %get-tuple-element.40), channel_id=1, source_target_pairs={{0,12},{1,13},{2,14},{3,15},{4,8},{5,9},{6,10},{7,11},{8,4},{9,5},... | collective-permute-start | bytes 215048 | tf_op jit(solution)/shard_map/ppermute | solution.py:444
  78.2 4.1 %collective-permute-start.26 = (bf16[8,2688]{1,0:T(8,128)(2,1)S(1)}, bf16[8,2688]{1,0:T(8,128)(2,1)S(1)}, u32[]{:S(2)}, u32[]{:S(2)}) collective-permute-start(bf16[8,2688]{1,0:T(8,128)(2,1)S(1)} %get-tuple-element.48), channel_id=1, source_target_pairs={{0,2},{1,3},{2,0},{3,1},{4,6},{5,7},{6,4},{7,5},{8,10},{9,11},{10,... | collective-permute-start | bytes 129032 | tf_op jit(solution)/shard_map/ppermute | solution.py:444

commit v2 on v1

--- a/solution.py
+++ b/solution.py
@@ -361,7 +361,7 @@
             whole_at = first + at
             fetch(whole_at).wait()
             result = jnp.dot(hidden_ref[...], near_ref[lax.rem(whole_at, slots)], preferred_element_type=F32)
-            weighted = (result.astype(BF16).astype(F32) * gate).astype(BF16)
+            weighted = (result * gate).astype(BF16)
             columns = pl.ds(pl.multiple_of(at * step, LANES), step)
             keep_ref[:, columns] = weighted[:half_rows]
             send_ref[:, columns] = weighted[half_rows:]
@@ -465,9 +465,10 @@
         across.append(swap(block, 2))
     same = along + across
     masks = [2 * k for k in range(line_count)] + [2 * k + 1 for k in range(line_count)]
-    beside = [swap(block, 1) for block in same]
 
     partial_value = shared_up(same, masks, near_up)
+    last, partial_value = lax.optimization_barrier((same[-1], partial_value))
+    beside = [swap(block, 1) for block in same[:-1] + [last]]
     width, features = tokens.shape[2], 2 * own_down.shape[0]
     unit = features if features % LANES == 0 else LANES
     first_width = (width // unit * FIRST_EIGHTHS + 4) // 8 * unit

time: 83.5 us -> 81.5 us (0.976)
  waiting for transfers between devices: 23.2 us -> 21.8 us
    ppermute x27, waiting for transfers between devices: 15.8 us -> 14.5 us  [swap(): lax.ppermute(value, 'expert', [(i, i ^ mask) for i in range(device_count)])]
    all_to_all x2, starting transfers between devices: 11.8 us -> 10.5 us  [exchange(): lax.all_to_all(value, 'expert', 0, 0, axis_index_groups=groups, tiled=True)]
  transfers between devices with their start and end apart: 29 -> 29, of which waited for: 7 -> 7; matrix products, arithmetic and copies ran while one was open for 0% -> 0% of each run, Pallas kernels for 29% -> 30%
where the time goes in v2:
time: 81.5 us; the launch traced here: 81.1 us
  starting transfers between devices  33.6 us (41%)
  Pallas kernels  24.7 us (30%)
  waiting for transfers between devices  21.8 us (27%)
    ppermute x27, starting transfers between devices, swap(): lax.ppermute(value, 'expert', [(i, i ^ mask) for i in range(device_count)])  23.1 us
    ppermute x27, waiting for transfers between devices, swap(): lax.ppermute(value, 'expert', [(i, i ^ mask) for i in range(device_count)])  14.5 us
    all_to_all x2, starting transfers between devices, exchange(): lax.all_to_all(value, 'expert', 0, 0, axis_index_groups=groups, tiled=True)  10.5 us
    pallas_call x1, Pallas kernels, routed_up(): pl.pallas_call(functools.partial(routed_up_kernel, len(blocks), expert_co...  10.3 us
    all_to_all x2, waiting for transfers between devices, exchange(): lax.all_to_all(value, 'expert', 0, 0, axis_index_groups=groups, tiled=True)  7.33 us
    pallas_call x1, Pallas kernels, routed_down(): pl.pallas_call(functools.partial(routed_down_kernel, step, len(widths)),...  6.6 us
    pallas_call x1, Pallas kernels, shared_down_rows(): pl.pallas_call(shared_down_kernel, out_shape=jax.ShapeDtypeStruct((count,...  1.87 us
  transfers between devices with their start and end apart: 29, of which 7 were waited for; matrix products, arithmetic and copies ran while one was open for 0% of the time, Pallas kernels for 30%

profile of v2, /device:TPU:0, one launch (start us, length us, event | category | flops | bytes accessed | tf_op | source)
XLA Modules:
  0.0 81.1 jit_solution(15898206454781560677)
XLA Ops:
  0.0 0.5 collective-permute-start.14
  0.5 1.2 %shard_map.91.refs_0_ = bf16[8,7296]{1,0:T(8,128)(2,1)S(1)} custom-call(s32[1,2]{1,0:T(1,128)} %bitcast.7, bf16[2,4,7168]{2,1,0:T(4,128)(2,1)} %tokens_ref.1, s32[1,2,4,8]{3,2,1,0:T(4,128)} %refs_2_.1, f32[1,2,4,8]{3,2,1,0:T(4,128)} %refs_3_.1, f32[1,7168]{1,0:T(1,128)} %refs_4_.1), custom_call_target="tpu_custom_call" | custom-call | flops 458752 | bytes 344064 | tf_op jit(solution)/shard_map/pallas_call | solution.py:92
  1.7 2.6 %collective-permute-start = (bf16[8,7296]{1,0:T(8,128)(2,1)S(1)}, bf16[8,7296]{1,0:T(8,128)(2,1)S(1)}, u32[]{:S(2)}, u32[]{:S(2)}) collective-permute-start(bf16[8,7296]{1,0:T(8,128)(2,1)S(1)} %shard_map.91.refs_0_), channel_id=1, source_target_pairs={{0,4},{1,5},{2,6},{3,7},{4,0},{5,1},{6,2},{7,3},{8,12},{9,13},{10,... | collective-permute-start | bytes 350216 | tf_op jit(solution)/shard_map/ppermute | solution.py:444
  4.3 2.6 %collective-permute-start.1 = (bf16[8,7296]{1,0:T(8,128)(2,1)S(1)}, bf16[8,7296]{1,0:T(8,128)(2,1)S(1)}, u32[]{:S(2)}, u32[]{:S(2)}) collective-permute-start(bf16[8,7296]{1,0:T(8,128)(2,1)S(1)} %shard_map.91.refs_0_), channel_id=1, source_target_pairs={{0,8},{1,9},{2,10},{3,11},{4,12},{5,13},{6,14},{7,15},{8,0},{9,1},... | collective-permute-start | bytes 350216 | tf_op jit(solution)/shard_map/ppermute | solution.py:444
  6.9 0.0 collective-permute-start.2
  6.9 1.7 %collective-permute-start.3 = (bf16[8,7296]{1,0:T(8,128)(2,1)S(1)}, bf16[8,7296]{1,0:T(8,128)(2,1)S(1)}, u32[]{:S(2)}, u32[]{:S(2)}) collective-permute-start(bf16[8,7296]{1,0:T(8,128)(2,1)S(1)} %shard_map.91.refs_0_), channel_id=1, source_target_pairs={{0,2},{1,3},{2,0},{3,1},{4,6},{5,7},{6,4},{7,5},{8,10},{9,11},{10,... | collective-permute-start | bytes 350216 | tf_op jit(solution)/shard_map/ppermute | solution.py:444
  8.6 1.3 %collective-permute-done.refs_1_ = bf16[8,7296]{1,0:T(8,128)(2,1)S(1)} collective-permute-done((bf16[8,7296]{1,0:T(8,128)(2,1)S(1)}, bf16[8,7296]{1,0:T(8,128)(2,1)S(1)}, u32[]{:S(2)}, u32[]{:S(2)}) %collective-permute-start) | collective-permute-done | bytes 116768 | tf_op jit(solution)/shard_map/ppermute | solution.py:444
  10.0 1.7 %collective-permute-start.4 = (bf16[8,7296]{1,0:T(8,128)(2,1)S(1)}, bf16[8,7296]{1,0:T(8,128)(2,1)S(1)}, u32[]{:S(2)}, u32[]{:S(2)}) collective-permute-start(bf16[8,7296]{1,0:T(8,128)(2,1)S(1)} %collective-permute-done.refs_1_), channel_id=1, source_target_pairs={{0,2},{1,3},{2,0},{3,1},{4,6},{5,7},{6,4},{7,5},{8,10},{9,11},{10,... | collective-permute-start | bytes 350216 | tf_op jit(solution)/shard_map/ppermute | solution.py:444
  11.7 4.6 %collective-permute-done.1.refs_2_ = bf16[8,7296]{1,0:T(8,128)(2,1)S(1)} collective-permute-done((bf16[8,7296]{1,0:T(8,128)(2,1)S(1)}, bf16[8,7296]{1,0:T(8,128)(2,1)S(1)}, u32[]{:S(2)}, u32[]{:S(2)}) %collective-permute-start.1) | collective-permute-done | bytes 116768 | tf_op jit(solution)/shard_map/ppermute | solution.py:444
  16.3 1.5 %collective-permute-start.5 = (bf16[8,7296]{1,0:T(8,128)(2,1)S(1)}, bf16[8,7296]{1,0:T(8,128)(2,1)S(1)}, u32[]{:S(2)}, u32[]{:S(2)}) collective-permute-start(bf16[8,7296]{1,0:T(8,128)(2,1)S(1)} %collective-permute-done.1.refs_2_), channel_id=1, source_target_pairs={{0,2},{1,3},{2,0},{3,1},{4,6},{5,7},{6,4},{7,5},{8,10},{9,11},{10,... | collective-permute-start | bytes 350216 | tf_op jit(solution)/shard_map/ppermute | solution.py:444
  17.8 0.0 collective-permute-done.2.refs_3_
  17.8 0.5 collective-permute-start.6
  18.3 0.0 collective-permute-done.3.refs_4_
  18.3 0.0 collective-permute-start.7
  18.3 0.0 collective-permute-done.4.refs_5_
  18.4 0.5 collective-permute-start.10
  18.9 0.0 collective-permute-done.14.other_hbm
  18.9 0.1 collective-permute-start.8
  18.9 1.5 %shard_map.92.refs_8_ = bf16[896,2048]{1,0:T(8,128)(2,1)S(1)} custom-call(bf16[448,2048]{1,0:T(8,128)(2,1)} %bitcast.12, bf16[448,2048]{1,0:T(8,128)(2,1)S(1)} %collective-permute-done.14.other_hbm), custom_call_target="tpu_custom_call" | custom-call | bytes 3670016 | tf_op jit(solution)/shard_map/pallas_call | solution.py:175
  20.5 0.7 collective-permute-done.5.refs_6_
  21.1 0.0 collective-permute-start.9
  21.1 1.5 %collective-permute-done.6.refs_7_ = bf16[8,7296]{1,0:T(8,128)(2,1)S(1)} collective-permute-done((bf16[8,7296]{1,0:T(8,128)(2,1)S(1)}, bf16[8,7296]{1,0:T(8,128)(2,1)S(1)}, u32[]{:S(2)}, u32[]{:S(2)}) %collective-permute-start.6) | collective-permute-done | bytes 116768 | tf_op jit(solution)/shard_map/ppermute | solution.py:444
  22.6 0.0 collective-permute-start.11
  22.6 1.5 %shard_map.93 = bf16[8,8,2048]{2,1,0:T(8,128)(2,1)} custom-call(bf16[8,7296]{1,0:T(8,128)(2,1)S(1)} %shard_map.91.refs_0_, bf16[8,7296]{1,0:T(8,128)(2,1)S(1)} %collective-permute-done.refs_1_, bf16[8,7296]{1,0:T(8,128)(2,1)S(1)} %collective-permute-done.1.refs_2_, bf16[8,7296]{1,0:T(8,128)(2,1)S(1)} %collective-permute-done.2.refs_3_, ...), custom_call_target="tpu_custom_call" | custom-call | flops 234881024 | bytes 3670016 | tf_op jit(solution)/shard_map/pallas_call | solution.py:206
  24.1 0.0 collective-permute-done.7.refs_8_
  24.1 0.5 collective-permute-start.12
  24.6 0.0 collective-permute-done.10.refs_11_
  24.6 0.1 collective-permute-start.13
  24.7 0.0 collective-permute-done.8.refs_9_
  24.7 0.4 collective-permute-start.15
  25.1 4.6 %all-to-all-start = ((bf16[8,8,2048]{2,1,0:T(8,128)(2,1)}), bf16[8,8,2048]{2,1,0:T(8,128)(2,1)S(1)}, u32[]{:S(2)}, u32[]{:S(2)}) async-start(bf16[8,8,2048]{2,1,0:T(8,128)(2,1)} %shard_map.93), calls=%async_computation | async-start | bytes 524288 | tf_op jit(solution)/shard_map/all_to_all | solution.py:455
  29.7 0.0 collective-permute-done.9.refs_10_
  29.7 0.1 collective-permute-start.17
  29.8 0.0 collective-permute-done.12.refs_13_
  29.8 0.0 collective-permute-done.13.refs_14_
  29.9 10.3 %shard_map.94 = (bf16[128,1024]{1,0:T(8,128)(2,1)S(1)}, f32[128,128]{1,0:T(8,128)S(1)}) custom-call(bf16[8,7296]{1,0:T(8,128)(2,1)S(1)} %shard_map.91.refs_0_, bf16[8,7296]{1,0:T(8,128)(2,1)S(1)} %collective-permute-done.refs_1_, bf16[8,7296]{1,0:T(8,128)(2,1)S(1)} %collective-permute-done.1.refs_2_, bf16[8,7296]{1,0:T(8,128)(2,1)S(1)} %collective-permute-done.2.refs_3_, ...), custom_call_target="tpu_custom_call" | custom-call | flops 3758096384 | bytes 29360128 | tf_op jit(solution)/shard_map/pallas_call | solution.py:323
  40.2 0.7 shard_map.95
  40.9 6.6 %shard_map.96 = (bf16[64,4480]{1,0:T(8,128)(2,1)S(1)}, bf16[64,4480]{1,0:T(8,128)(2,1)}, bf16[64,2688]{1,0:T(8,128)(2,1)S(1)}, bf16[64,2688]{1,0:T(8,128)(2,1)S(1)}) custom-call(bf16[128,1024]{1,0:T(8,128)(2,1)S(1)} %get-tuple-element.32.hidden_ref, f32[128,128]{1,0:T(8,128)S(1)} %get-tuple-element.33.gate_ref, bf16[1024,7168]{1,0:T(8,128)(2,1)} %bitcast.10), custom_call_target="tpu_custom_call" | custom-call | flops 1879048192 | bytes 14680064 | tf_op jit(solution)/shard_map/pallas_call | solution.py:383
  47.5 0.8 copy-done.2
  48.2 0.5 collective-permute-start.16
  48.7 5.9 %all-to-all-start.1 = ((bf16[8,8,1024]{2,1,0:T(8,128)(2,1)}), bf16[8,8,1024]{2,1,0:T(8,128)(2,1)S(1)}, u32[]{:S(2)}, u32[]{:S(2)}) async-start(bf16[8,8,1024]{2,1,0:T(8,128)(2,1)} %shard_map.95), calls=%async_computation.1 | async-start | bytes 262144 | tf_op jit(solution)/shard_map/all_to_all | solution.py:455
  54.6 7.3 %all-to-all-done.1.blocks_ref = bf16[8,8,1024]{2,1,0:T(8,128)(2,1)S(1)} async-done(((bf16[8,8,1024]{2,1,0:T(8,128)(2,1)}), bf16[8,8,1024]{2,1,0:T(8,128)(2,1)S(1)}, u32[]{:S(2)}, u32[]{:S(2)}) %all-to-all-start.1) | async-done | bytes 131104 | tf_op jit(solution)/shard_map/all_to_all | solution.py:455
  62.0 1.9 %shard_map.97.refs_2_ = bf16[8,8,896]{2,1,0:T(8,128)(2,1)S(1)} custom-call(bf16[8,8,1024]{2,1,0:T(8,128)(2,1)S(1)} %all-to-all-done.1.blocks_ref, bf16[448,1024]{1,0:T(8,128)(2,1)} %bitcast.14, bf16[448,1024]{1,0:T(8,128)(2,1)S(1)} %collective-permute-done.17.other_hbm), custom_call_target="tpu_custom_call" | custom-call | flops 117440512 | bytes 1835008 | tf_op jit(solution)/shard_map/pallas_call | solution.py:237
  63.9 0.0 collective-permute-done.16.refs_1_
  63.9 0.2 shard_map.98
  64.0 0.4 collective-permute-start.18
  64.5 0.0 collective-permute-done.22.refs_1_
  64.5 0.1 shard_map.100
  64.6 1.0 %collective-permute-start.23 = (bf16[16,2688]{1,0:T(8,128)(2,1)S(1)}, bf16[16,2688]{1,0:T(8,128)(2,1)S(1)}, u32[]{:S(2)}, u32[]{:S(2)}) collective-permute-start(bf16[16,2688]{1,0:T(8,128)(2,1)S(1)} %get-tuple-element.48), channel_id=1, source_target_pairs={{0,4},{1,5},{2,6},{3,7},{4,0},{5,1},{6,2},{7,3},{8,12},{9,13},{10,... | collective-permute-start | bytes 258056 | tf_op jit(solution)/shard_map/ppermute | solution.py:444
  65.6 1.2 %collective-permute-start.24 = (bf16[16,2688]{1,0:T(8,128)(2,1)S(1)}, bf16[16,2688]{1,0:T(8,128)(2,1)S(1)}, u32[]{:S(2)}, u32[]{:S(2)}) collective-permute-start(bf16[16,2688]{1,0:T(8,128)(2,1)S(1)} %get-tuple-element.49), channel_id=1, source_target_pairs={{0,8},{1,9},{2,10},{3,11},{4,12},{5,13},{6,14},{7,15},{8,0},{9,1},... | collective-permute-start | bytes 258056 | tf_op jit(solution)/shard_map/ppermute | solution.py:444
  66.8 2.2 %collective-permute-start.25 = (bf16[16,2688]{1,0:T(8,128)(2,1)S(1)}, bf16[16,2688]{1,0:T(8,128)(2,1)S(1)}, u32[]{:S(2)}, u32[]{:S(2)}) collective-permute-start(bf16[16,2688]{1,0:T(8,128)(2,1)S(1)} %get-tuple-element.50), channel_id=1, source_target_pairs={{0,12},{1,13},{2,14},{3,15},{4,8},{5,9},{6,10},{7,11},{8,4},{9,5},... | collective-permute-start | bytes 258056 | tf_op jit(solution)/shard_map/ppermute | solution.py:444
  69.0 2.6 %collective-permute-done.18.refs_1_ = bf16[32,4480]{1,0:T(8,128)(2,1)S(1)} collective-permute-done((bf16[32,4480]{1,0:T(8,128)(2,1)S(1)}, bf16[32,4480]{1,0:T(8,128)(2,1)S(1)}, u32[]{:S(2)}, u32[]{:S(2)}) %collective-permute-start.18) | collective-permute-done | bytes 286752 | tf_op jit(solution)/shard_map/ppermute | solution.py:444
  71.6 0.1 shard_map.99
  71.7 0.2 collective-permute-start.19
  71.9 1.7 %collective-permute-start.20 = (bf16[8,4480]{1,0:T(8,128)(2,1)S(1)}, bf16[8,4480]{1,0:T(8,128)(2,1)S(1)}, u32[]{:S(2)}, u32[]{:S(2)}) collective-permute-start(bf16[8,4480]{1,0:T(8,128)(2,1)S(1)} %get-tuple-element.43), channel_id=1, source_target_pairs={{0,8},{1,9},{2,10},{3,11},{4,12},{5,13},{6,14},{7,15},{8,0},{9,1},... | collective-permute-start | bytes 215048 | tf_op jit(solution)/shard_map/ppermute | solution.py:444
  73.6 0.0 collective-permute-done.23.refs_1_
  73.6 2.5 %collective-permute-start.21 = (bf16[8,4480]{1,0:T(8,128)(2,1)S(1)}, bf16[8,4480]{1,0:T(8,128)(2,1)S(1)}, u32[]{:S(2)}, u32[]{:S(2)}) collective-permute-start(bf16[8,4480]{1,0:T(8,128)(2,1)S(1)} %get-tuple-element.44), channel_id=1, source_target_pairs={{0,12},{1,13},{2,14},{3,15},{4,8},{5,9},{6,10},{7,11},{8,4},{9,5},... | collective-permute-start | bytes 215048 | tf_op jit(solution)/shard_map/ppermute | solution.py:444
  76.1 0.0 collective-permute-done.24.refs_2_
  76.2 0.4 collective-permute-start.26
  76.5 3.7 %collective-permute-done.26.refs_5_ = bf16[8,2688]{1,0:T(8,128)(2,1)S(1)} collective-permute-done((bf16[8,2688]{1,0:T(8,128)(2,1)S(1)}, bf16[8,2688]{1,0:T(8,128)(2,1)S(1)}, u32[]{:S(2)}, u32[]{:S(2)}) %collective-permute-start.26) | collective-permute-done | bytes 43040 | tf_op jit(solution)/shard_map/ppermute | solution.py:444
  80.3 0.0 collective-permute-done.19.refs_1_
  80.3 0.0 collective-permute-done.20.refs_2_
  80.3 0.0 collective-permute-done.21.refs_3_
  80.3 0.8 shard_map.102
  (12 shorter events, 0.1 us)
Async XLA Ops:
  0.0 18.9 %collective-permute-start.14 = (bf16[448,2048]{1,0:T(8,128)(2,1)}, bf16[448,2048]{1,0:T(8,128)(2,1)S(1)}, u32[]{:S(2)}, u32[]{:S(2)}) collective-permute-start(bf16[448,2048]{1,0:T(8,128)(2,1)} %bitcast.11), channel_id=1, source_target_pairs={{0,1},{1,0},{2,3},{3,2},{4,5},{5,4},{6,7},{7,6},{8,9},{9,8},{10,11... | collective-permute-start | bytes 5505032 | tf_op jit(solution)/shard_map/ppermute | solution.py:444
  1.7 8.3 %collective-permute-start = (bf16[8,7296]{1,0:T(8,128)(2,1)S(1)}, bf16[8,7296]{1,0:T(8,128)(2,1)S(1)}, u32[]{:S(2)}, u32[]{:S(2)}) collective-permute-start(bf16[8,7296]{1,0:T(8,128)(2,1)S(1)} %shard_map.91.refs_0_), channel_id=1, source_target_pairs={{0,4},{1,5},{2,6},{3,7},{4,0},{5,1},{6,2},{7,3},{8,12},{9,13},{10,... | collective-permute-start | bytes 350216 | tf_op jit(solution)/shard_map/ppermute | solution.py:444
  4.3 12.0 %collective-permute-start.1 = (bf16[8,7296]{1,0:T(8,128)(2,1)S(1)}, bf16[8,7296]{1,0:T(8,128)(2,1)S(1)}, u32[]{:S(2)}, u32[]{:S(2)}) collective-permute-start(bf16[8,7296]{1,0:T(8,128)(2,1)S(1)} %shard_map.91.refs_0_), channel_id=1, source_target_pairs={{0,8},{1,9},{2,10},{3,11},{4,12},{5,13},{6,14},{7,15},{8,0},{9,1},... | collective-permute-start | bytes 350216 | tf_op jit(solution)/shard_map/ppermute | solution.py:444
  6.9 10.9 %collective-permute-start.2 = (bf16[8,7296]{1,0:T(8,128)(2,1)S(1)}, bf16[8,7296]{1,0:T(8,128)(2,1)S(1)}, u32[]{:S(2)}, u32[]{:S(2)}) collective-permute-start(bf16[8,7296]{1,0:T(8,128)(2,1)S(1)} %shard_map.91.refs_0_), channel_id=1, source_target_pairs={{0,12},{1,13},{2,14},{3,15},{4,8},{5,9},{6,10},{7,11},{8,4},{9,5},... | collective-permute-start | bytes 350216 | tf_op jit(solution)/shard_map/ppermute | solution.py:444
  6.9 11.5 %collective-permute-start.3 = (bf16[8,7296]{1,0:T(8,128)(2,1)S(1)}, bf16[8,7296]{1,0:T(8,128)(2,1)S(1)}, u32[]{:S(2)}, u32[]{:S(2)}) collective-permute-start(bf16[8,7296]{1,0:T(8,128)(2,1)S(1)} %shard_map.91.refs_0_), channel_id=1, source_target_pairs={{0,2},{1,3},{2,0},{3,1},{4,6},{5,7},{6,4},{7,5},{8,10},{9,11},{10,... | collective-permute-start | bytes 350216 | tf_op jit(solution)/shard_map/ppermute | solution.py:444
  10.0 8.4 %collective-permute-start.4 = (bf16[8,7296]{1,0:T(8,128)(2,1)S(1)}, bf16[8,7296]{1,0:T(8,128)(2,1)S(1)}, u32[]{:S(2)}, u32[]{:S(2)}) collective-permute-start(bf16[8,7296]{1,0:T(8,128)(2,1)S(1)} %collective-permute-done.refs_1_), channel_id=1, source_target_pairs={{0,2},{1,3},{2,0},{3,1},{4,6},{5,7},{6,4},{7,5},{8,10},{9,11},{10,... | collective-permute-start | bytes 350216 | tf_op jit(solution)/shard_map/ppermute | solution.py:444
  16.3 4.8 %collective-permute-start.5 = (bf16[8,7296]{1,0:T(8,128)(2,1)S(1)}, bf16[8,7296]{1,0:T(8,128)(2,1)S(1)}, u32[]{:S(2)}, u32[]{:S(2)}) collective-permute-start(bf16[8,7296]{1,0:T(8,128)(2,1)S(1)} %collective-permute-done.1.refs_2_), channel_id=1, source_target_pairs={{0,2},{1,3},{2,0},{3,1},{4,6},{5,7},{6,4},{7,5},{8,10},{9,11},{10,... | collective-permute-start | bytes 350216 | tf_op jit(solution)/shard_map/ppermute | solution.py:444
  17.8 4.8 %collective-permute-start.6 = (bf16[8,7296]{1,0:T(8,128)(2,1)S(1)}, bf16[8,7296]{1,0:T(8,128)(2,1)S(1)}, u32[]{:S(2)}, u32[]{:S(2)}) collective-permute-start(bf16[8,7296]{1,0:T(8,128)(2,1)S(1)} %collective-permute-done.2.refs_3_), channel_id=1, source_target_pairs={{0,2},{1,3},{2,0},{3,1},{4,6},{5,7},{6,4},{7,5},{8,10},{9,11},{10,... | collective-permute-start | bytes 350216 | tf_op jit(solution)/shard_map/ppermute | solution.py:444
  18.3 5.8 %collective-permute-start.7 = (bf16[8,7296]{1,0:T(8,128)(2,1)S(1)}, bf16[8,7296]{1,0:T(8,128)(2,1)S(1)}, u32[]{:S(2)}, u32[]{:S(2)}) collective-permute-start(bf16[8,7296]{1,0:T(8,128)(2,1)S(1)} %shard_map.91.refs_0_), channel_id=1, source_target_pairs={{0,1},{1,0},{2,3},{3,2},{4,5},{5,4},{6,7},{7,6},{8,9},{9,8},{10,11... | collective-permute-start | bytes 350216 | tf_op jit(solution)/shard_map/ppermute | solution.py:444
  18.4 6.3 %collective-permute-start.10 = (bf16[8,7296]{1,0:T(8,128)(2,1)S(1)}, bf16[8,7296]{1,0:T(8,128)(2,1)S(1)}, u32[]{:S(2)}, u32[]{:S(2)}) collective-permute-start(bf16[8,7296]{1,0:T(8,128)(2,1)S(1)} %collective-permute-done.2.refs_3_), channel_id=1, source_target_pairs={{0,1},{1,0},{2,3},{3,2},{4,5},{5,4},{6,7},{7,6},{8,9},{9,8},{10,11... | collective-permute-start | bytes 350216 | tf_op jit(solution)/shard_map/ppermute | solution.py:444
  18.9 5.8 %collective-permute-start.8 = (bf16[8,7296]{1,0:T(8,128)(2,1)S(1)}, bf16[8,7296]{1,0:T(8,128)(2,1)S(1)}, u32[]{:S(2)}, u32[]{:S(2)}) collective-permute-start(bf16[8,7296]{1,0:T(8,128)(2,1)S(1)} %collective-permute-done.refs_1_), channel_id=1, source_target_pairs={{0,1},{1,0},{2,3},{3,2},{4,5},{5,4},{6,7},{7,6},{8,9},{9,8},{10,11... | collective-permute-start | bytes 350216 | tf_op jit(solution)/shard_map/ppermute | solution.py:444
  21.1 8.6 %collective-permute-start.9 = (bf16[8,7296]{1,0:T(8,128)(2,1)S(1)}, bf16[8,7296]{1,0:T(8,128)(2,1)S(1)}, u32[]{:S(2)}, u32[]{:S(2)}) collective-permute-start(bf16[8,7296]{1,0:T(8,128)(2,1)S(1)} %collective-permute-done.1.refs_2_), channel_id=1, source_target_pairs={{0,1},{1,0},{2,3},{3,2},{4,5},{5,4},{6,7},{7,6},{8,9},{9,8},{10,11... | collective-permute-start | bytes 350216 | tf_op jit(solution)/shard_map/ppermute | solution.py:444
  22.6 7.2 %collective-permute-start.11 = (bf16[8,7296]{1,0:T(8,128)(2,1)S(1)}, bf16[8,7296]{1,0:T(8,128)(2,1)S(1)}, u32[]{:S(2)}, u32[]{:S(2)}) collective-permute-start(bf16[8,7296]{1,0:T(8,128)(2,1)S(1)} %collective-permute-done.3.refs_4_), channel_id=1, source_target_pairs={{0,1},{1,0},{2,3},{3,2},{4,5},{5,4},{6,7},{7,6},{8,9},{9,8},{10,11... | collective-permute-start | bytes 350216 | tf_op jit(solution)/shard_map/ppermute | solution.py:444
  24.1 5.7 %collective-permute-start.12 = (bf16[8,7296]{1,0:T(8,128)(2,1)S(1)}, bf16[8,7296]{1,0:T(8,128)(2,1)S(1)}, u32[]{:S(2)}, u32[]{:S(2)}) collective-permute-start(bf16[8,7296]{1,0:T(8,128)(2,1)S(1)} %collective-permute-done.4.refs_5_), channel_id=1, source_target_pairs={{0,1},{1,0},{2,3},{3,2},{4,5},{5,4},{6,7},{7,6},{8,9},{9,8},{10,11... | collective-permute-start | bytes 350216 | tf_op jit(solution)/shard_map/ppermute | solution.py:444
  24.6 5.2 %collective-permute-start.13 = (bf16[8,7296]{1,0:T(8,128)(2,1)S(1)}, bf16[8,7296]{1,0:T(8,128)(2,1)S(1)}, u32[]{:S(2)}, u32[]{:S(2)}) collective-permute-start(bf16[8,7296]{1,0:T(8,128)(2,1)S(1)} %collective-permute-done.5.refs_6_), channel_id=1, source_target_pairs={{0,1},{1,0},{2,3},{3,2},{4,5},{5,4},{6,7},{7,6},{8,9},{9,8},{10,11... | collective-permute-start | bytes 350216 | tf_op jit(solution)/shard_map/ppermute | solution.py:444
  24.7 5.2 %collective-permute-start.15 = (bf16[8,7296]{1,0:T(8,128)(2,1)S(1)}, bf16[8,7296]{1,0:T(8,128)(2,1)S(1)}, u32[]{:S(2)}, u32[]{:S(2)}) collective-permute-start(bf16[8,7296]{1,0:T(8,128)(2,1)S(1)} %collective-permute-done.6.refs_7_), channel_id=1, source_target_pairs={{0,1},{1,0},{2,3},{3,2},{4,5},{5,4},{6,7},{7,6},{8,9},{9,8},{10,11... | collective-permute-start | bytes 350216 | tf_op jit(solution)/shard_map/ppermute | solution.py:444
  25.1 15.0 %all-to-all-start = ((bf16[8,8,2048]{2,1,0:T(8,128)(2,1)}), bf16[8,8,2048]{2,1,0:T(8,128)(2,1)S(1)}, u32[]{:S(2)}, u32[]{:S(2)}) async-start(bf16[8,8,2048]{2,1,0:T(8,128)(2,1)} %shard_map.93), calls=%async_computation | async-start | bytes 524288 | tf_op jit(solution)/shard_map/all_to_all | solution.py:455
  29.7 24.9 %collective-permute-start.17 = (bf16[448,1024]{1,0:T(8,128)(2,1)}, bf16[448,1024]{1,0:T(8,128)(2,1)S(1)}, u32[]{:S(2)}, u32[]{:S(2)}) collective-permute-start(bf16[448,1024]{1,0:T(8,128)(2,1)} %bitcast.13), channel_id=1, source_target_pairs={{0,1},{1,0},{2,3},{3,2},{4,5},{5,4},{6,7},{7,6},{8,9},{9,8},{10,11... | collective-permute-start | bytes 2752520 | tf_op jit(solution)/shard_map/ppermute | solution.py:444
  47.5 0.8 copy-start.2
  48.2 32.1 %copy-start = (bf16[2,4,7168]{2,1,0:T(4,128)(2,1)S(1)}, bf16[2,4,7168]{2,1,0:T(4,128)(2,1)}, u32[]{:S(2)}) copy-start(bf16[2,4,7168]{2,1,0:T(4,128)(2,1)} %tokens_ref.1) | copy-start | bytes 344068
  48.2 32.1 %copy-start.1 = (s32[2,1]{0,1:T(1,128)S(1)}, s32[2,1]{0,1:T(1,128)}, u32[]{:S(2)}) copy-start(s32[2,1]{0,1:T(1,128)} %param.10) | copy-start | bytes 28
  48.2 15.6 %collective-permute-start.16 = (bf16[64,4480]{1,0:T(8,128)(2,1)}, bf16[64,4480]{1,0:T(8,128)(2,1)S(1)}, u32[]{:S(2)}, u32[]{:S(2)}) collective-permute-start(bf16[64,4480]{1,0:T(8,128)(2,1)} %get-tuple-element.37), channel_id=1, source_target_pairs={{0,1},{1,0},{2,3},{3,2},{4,5},{5,4},{6,7},{7,6},{8,9},{9,8},{10,11... | collective-permute-start | bytes 1720328 | tf_op jit(solution)/shard_map/ppermute | solution.py:444
  48.7 13.3 %all-to-all-start.1 = ((bf16[8,8,1024]{2,1,0:T(8,128)(2,1)}), bf16[8,8,1024]{2,1,0:T(8,128)(2,1)S(1)}, u32[]{:S(2)}, u32[]{:S(2)}) async-start(bf16[8,8,1024]{2,1,0:T(8,128)(2,1)} %shard_map.95), calls=%async_computation.1 | async-start | bytes 262144 | tf_op jit(solution)/shard_map/all_to_all | solution.py:455
  54.6 9.8 %collective-permute-start.22 = (bf16[64,2688]{1,0:T(8,128)(2,1)}, bf16[64,2688]{1,0:T(8,128)(2,1)S(1)}, u32[]{:S(2)}, u32[]{:S(2)}) collective-permute-start(bf16[64,2688]{1,0:T(8,128)(2,1)} %copy-done.2), channel_id=1, source_target_pairs={{0,1},{1,0},{2,3},{3,2},{4,5},{5,4},{6,7},{7,6},{8,9},{9,8},{10,11... | collective-permute-start | bytes 1032200 | tf_op jit(solution)/shard_map/ppermute | solution.py:444
  64.0 7.5 %collective-permute-start.18 = (bf16[32,4480]{1,0:T(8,128)(2,1)S(1)}, bf16[32,4480]{1,0:T(8,128)(2,1)S(1)}, u32[]{:S(2)}, u32[]{:S(2)}) collective-permute-start(bf16[32,4480]{1,0:T(8,128)(2,1)S(1)} %get-tuple-element.40), channel_id=1, source_target_pairs={{0,2},{1,3},{2,0},{3,1},{4,6},{5,7},{6,4},{7,5},{8,10},{9,11},{10,... | collective-permute-start | bytes 860168 | tf_op jit(solution)/shard_map/ppermute | solution.py:444
  64.6 9.0 %collective-permute-start.23 = (bf16[16,2688]{1,0:T(8,128)(2,1)S(1)}, bf16[16,2688]{1,0:T(8,128)(2,1)S(1)}, u32[]{:S(2)}, u32[]{:S(2)}) collective-permute-start(bf16[16,2688]{1,0:T(8,128)(2,1)S(1)} %get-tuple-element.48), channel_id=1, source_target_pairs={{0,4},{1,5},{2,6},{3,7},{4,0},{5,1},{6,2},{7,3},{8,12},{9,13},{10,... | collective-permute-start | bytes 258056 | tf_op jit(solution)/shard_map/ppermute | solution.py:444
  65.6 10.5 %collective-permute-start.24 = (bf16[16,2688]{1,0:T(8,128)(2,1)S(1)}, bf16[16,2688]{1,0:T(8,128)(2,1)S(1)}, u32[]{:S(2)}, u32[]{:S(2)}) collective-permute-start(bf16[16,2688]{1,0:T(8,128)(2,1)S(1)} %get-tuple-element.49), channel_id=1, source_target_pairs={{0,8},{1,9},{2,10},{3,11},{4,12},{5,13},{6,14},{7,15},{8,0},{9,1},... | collective-permute-start | bytes 258056 | tf_op jit(solution)/shard_map/ppermute | solution.py:444
  66.8 9.3 %collective-permute-start.25 = (bf16[16,2688]{1,0:T(8,128)(2,1)S(1)}, bf16[16,2688]{1,0:T(8,128)(2,1)S(1)}, u32[]{:S(2)}, u32[]{:S(2)}) collective-permute-start(bf16[16,2688]{1,0:T(8,128)(2,1)S(1)} %get-tuple-element.50), channel_id=1, source_target_pairs={{0,12},{1,13},{2,14},{3,15},{4,8},{5,9},{6,10},{7,11},{8,4},{9,5},... | collective-permute-start | bytes 258056 | tf_op jit(solution)/shard_map/ppermute | solution.py:444
  71.7 8.6 %collective-permute-start.19 = (bf16[8,4480]{1,0:T(8,128)(2,1)S(1)}, bf16[8,4480]{1,0:T(8,128)(2,1)S(1)}, u32[]{:S(2)}, u32[]{:S(2)}) collective-permute-start(bf16[8,4480]{1,0:T(8,128)(2,1)S(1)} %get-tuple-element.42), channel_id=1, source_target_pairs={{0,4},{1,5},{2,6},{3,7},{4,0},{5,1},{6,2},{7,3},{8,12},{9,13},{10,... | collective-permute-start | bytes 215048 | tf_op jit(solution)/shard_map/ppermute | solution.py:444
  71.9 8.4 %collective-permute-start.20 = (bf16[8,4480]{1,0:T(8,128)(2,1)S(1)}, bf16[8,4480]{1,0:T(8,128)(2,1)S(1)}, u32[]{:S(2)}, u32[]{:S(2)}) collective-permute-start(bf16[8,4480]{1,0:T(8,128)(2,1)S(1)} %get-tuple-element.43), channel_id=1, source_target_pairs={{0,8},{1,9},{2,10},{3,11},{4,12},{5,13},{6,14},{7,15},{8,0},{9,1},... | collective-permute-start | bytes 215048 | tf_op jit(solution)/shard_map/ppermute | solution.py:444
  73.6 6.7 %collective-permute-start.21 = (bf16[8,4480]{1,0:T(8,128)(2,1)S(1)}, bf16[8,4480]{1,0:T(8,128)(2,1)S(1)}, u32[]{:S(2)}, u32[]{:S(2)}) collective-permute-start(bf16[8,4480]{1,0:T(8,128)(2,1)S(1)} %get-tuple-element.44), channel_id=1, source_target_pairs={{0,12},{1,13},{2,14},{3,15},{4,8},{5,9},{6,10},{7,11},{8,4},{9,5},... | collective-permute-start | bytes 215048 | tf_op jit(solution)/shard_map/ppermute | solution.py:444
  76.2 4.1 %collective-permute-start.26 = (bf16[8,2688]{1,0:T(8,128)(2,1)S(1)}, bf16[8,2688]{1,0:T(8,128)(2,1)S(1)}, u32[]{:S(2)}, u32[]{:S(2)}) collective-permute-start(bf16[8,2688]{1,0:T(8,128)(2,1)S(1)} %get-tuple-element.52), channel_id=1, source_target_pairs={{0,2},{1,3},{2,0},{3,1},{4,6},{5,7},{6,4},{7,5},{8,10},{9,11},{10,... | collective-permute-start | bytes 129032 | tf_op jit(solution)/shard_map/ppermute | solution.py:444
